TPU v7x, 256 devices: a whole 4x4x8 slice. The times are simulated.
256 devices in a mesh: expert: 128 (over y, x, z), dp: 2 (over core).
Axes of the slice: x: 4, y: 4, z: 8, core: 2. Of those that a mesh axis runs over, the one named last changes fastest.
Arguments:
- tokens: bfloat16 [4096, 2048], P(('dp', 'expert')), parts along dimension 0, may hold values from -6 to 6
- expert_ids: int32 [4096, 8], P(('dp', 'expert')), parts along dimension 0, may hold values from 0 to 127, all different within a row; in each aligned block of 16 rows (0 to 15, 16 to 31, ...) at most 2 rows name the same one
- gate_values: float32 [4096, 8], P(('dp', 'expert')), parts along dimension 0, may hold values from 0.03 to 0.4
- w_gate: bfloat16 [128, 2048, 768], P('expert'), may hold values from -0.125 to 0.125
- w_up: bfloat16 [128, 2048, 768], P('expert'), may hold values from -0.125 to 0.125
- w_down: bfloat16 [128, 768, 2048], P('expert'), may hold values from -0.21875 to 0.21875
- cotangent: bfloat16 [4096, 2048], P(('dp', 'expert')), parts along dimension 0, may hold values from -6 to 6
Outputs:
- mixed_rows: bfloat16 [4096, 2048], P(('dp', 'expert')), parts along dimension 0
- row_grads: bfloat16 [4096, 2048], P(('dp', 'expert')), parts along dimension 0
- gate_grads: float32 [4096, 8], P(('dp', 'expert')), parts along dimension 0
There are 2 independent parts, one for each index of `dp`. A program takes and returns all parts, laid end to end along the dimension named above; an argument that names none is the same for every part. Nothing has to cross between parts.
Inputs may be any that keep to these rules, and one draw needn't show every extreme that they name: `expert_ids`: each token names 8 different experts. Among the 16 tokens of one device no expert is named more than 2 times, and in every draw some device names some expert exactly 2 times.
All inputs are finite; a program needn't handle non-finite values.
Results may differ from a plain program's by a relative error of at most 0.0064.
Values may be sent and summed in bfloat16 or wider, within the bound.
No kernel may reach another device: no remote copies, remote signals or barrier semaphores. Data moves between devices by JAX's collectives and lax.ppermute only.
A program may use at most 128 MiB of HBM per device.

v0:
```python
import jax
import jax.numpy as jnp
from jax import lax
from jax.sharding import PartitionSpec as P


def expert_forward(inputs, gate_matrix, up_matrix, down_matrix):
    pre_gate = jnp.dot(inputs, gate_matrix, preferred_element_type=jnp.float32)
    pre_up = jnp.dot(inputs, up_matrix, preferred_element_type=jnp.float32)
    hidden = (pre_gate * jax.nn.sigmoid(pre_gate) * pre_up).astype(jnp.bfloat16)
    output = jnp.dot(hidden, down_matrix, preferred_element_type=jnp.float32).astype(jnp.bfloat16)
    return (output, pre_gate, pre_up)


def expert_backward(grad_output, pre_gate, pre_up, gate_matrix, up_matrix, down_matrix):
    contract = (((1,), (1,)), ((), ()))
    grad_hidden = lax.dot_general(
        grad_output, down_matrix, contract, preferred_element_type=jnp.float32
    )
    sigmoid = jax.nn.sigmoid(pre_gate)
    grad_gate = (grad_hidden * pre_up * sigmoid * (1.0 + pre_gate * (1.0 - sigmoid))).astype(
        jnp.bfloat16
    )
    grad_up = (grad_hidden * pre_gate * sigmoid).astype(jnp.bfloat16)
    first_part = lax.dot_general(
        grad_gate, gate_matrix, contract, preferred_element_type=jnp.float32
    )
    second_part = lax.dot_general(grad_up, up_matrix, contract, preferred_element_type=jnp.float32)
    return (first_part + second_part).astype(jnp.bfloat16)


def slot_places(expert_ids, experts, capacity):
    flat_ids = expert_ids.reshape(-1)
    matches = (flat_ids[:, None] == jnp.arange(experts, dtype=jnp.int32)[None, :]).astype(jnp.int32)
    ranked = jnp.sum((jnp.cumsum(matches, axis=0) - matches) * matches, axis=1)
    return flat_ids * capacity + ranked


def local(tokens, expert_ids, gate_values, w_gate, w_up, w_down, cotangent):
    row_count, model_width = tokens.shape
    top_count = expert_ids.shape[1]
    experts = lax.axis_size("expert")
    capacity = max(2, 2 * row_count * top_count // experts)
    slot_total = experts * capacity
    entry_count = row_count * top_count
    gate_matrix = w_gate[0]
    up_matrix = w_up[0]
    down_matrix = w_down[0]
    places = slot_places(expert_ids, experts, capacity)
    flat_gates = gate_values.reshape(-1)
    upstream = jnp.repeat(cotangent, top_count, axis=0)
    padding = jnp.zeros((1, model_width), jnp.bfloat16)
    gathered_ids = lax.all_gather(expert_ids, "expert", axis=0, tiled=True)
    all_gates = lax.all_gather(gate_values, "expert", axis=0, tiled=True)
    all_tokens, all_cotangent = (
        lax.all_gather(tokens, "expert", axis=0, tiled=True),
        lax.all_gather(cotangent, "expert", axis=0, tiled=True),
    )
    own_expert = lax.axis_index("expert")
    all_flat = gathered_ids.reshape(experts, entry_count)
    matches = (all_flat == own_expert).astype(jnp.int32)
    ranked = jnp.cumsum(matches, axis=1) - matches
    sources = jnp.arange(experts, dtype=jnp.int32)[:, None]
    placed = jnp.where(matches == 1, sources * capacity + ranked, slot_total)
    entries = sources * entry_count + jnp.arange(entry_count, dtype=jnp.int32)[None, :]
    slot_table = (
        jnp.full((slot_total + 1,), experts * entry_count, jnp.int32)
        .at[placed.reshape(-1)]
        .set(entries.reshape(-1))[:slot_total]
    )
    token_of = slot_table // top_count
    received = jnp.concatenate([all_tokens, padding], axis=0)[token_of]
    output, pre_gate, pre_up = expert_forward(received, gate_matrix, up_matrix, down_matrix)
    slot_gates = jnp.concatenate([all_gates.reshape(-1), jnp.zeros((1,), jnp.float32)])[slot_table]
    chosen = jnp.concatenate([all_cotangent, padding], axis=0)[token_of]
    incoming = (slot_gates[:, None] * chosen.astype(jnp.float32)).astype(jnp.bfloat16)
    grad_rows = expert_backward(incoming, pre_gate, pre_up, gate_matrix, up_matrix, down_matrix)
    returned = lax.all_to_all(
        output.reshape(experts, capacity, model_width),
        "expert",
        split_axis=0,
        concat_axis=0,
        tiled=True,
    ).reshape(slot_total, model_width)
    returned_grads = lax.all_to_all(
        grad_rows.reshape(experts, capacity, model_width),
        "expert",
        split_axis=0,
        concat_axis=0,
        tiled=True,
    ).reshape(slot_total, model_width)
    picked = returned[places]
    weighted = flat_gates[:, None] * picked.astype(jnp.float32)
    mixed_rows = jnp.sum(weighted.reshape(row_count, top_count, model_width), axis=1).astype(
        jnp.bfloat16
    )
    gate_grads = jnp.einsum(
        "jd,jd->j", upstream, picked, preferred_element_type=jnp.float32
    ).reshape(row_count, top_count)
    picked_grads = returned_grads[places].astype(jnp.float32)
    row_grads = jnp.sum(picked_grads.reshape(row_count, top_count, model_width), axis=1).astype(
        jnp.bfloat16
    )
    return (mixed_rows, row_grads, gate_grads)


def solution(mesh):
    return jax.shard_map(
        local,
        mesh=mesh,
        in_specs=(
            P(("dp", "expert"), None),
            P(("dp", "expert"), None),
            P(("dp", "expert"), None),
            P("expert", None, None),
            P("expert", None, None),
            P("expert", None, None),
            P(("dp", "expert"), None),
        ),
        out_specs=(P(("dp", "expert"), None), P(("dp", "expert"), None), P(("dp", "expert"), None)),
        check_vma=False,
    )
```

profile of v0, /device:TPU:32, one launch (start us, length us, event | category | flops | bytes accessed | tf_op | source)
XLA Modules:
  0.0 932.4 jit_solution(493597241722205819)
XLA Ops:
  8.7 366.2 %all-gather = s32[128,16,8]{1,2,0:T(8,128)} all-gather(s32[1,16,8]{1,2,0:T(8,128)} %bitcast.48), channel_id=1, replica_groups=mesh['expert'=128,'dp'=2] {'expert'}, dimensions={0}, use_global_device_ids=true | all-gather | bytes 66048 | tf_op jit(solution)/shard_map/all_gather | solution.py:53
  379.5 367.1 %all-gather.1 = f32[128,16,8]{1,2,0:T(8,128)} all-gather(f32[1,16,8]{1,2,0:T(8,128)S(1)} %bitcast.49), channel_id=1, replica_groups=mesh['expert'=128,'dp'=2] {'expert'}, dimensions={0}, use_global_device_ids=true | all-gather | bytes 66048 | tf_op jit(solution)/shard_map/all_gather | solution.py:54
  746.6 2.4 copy.28
  751.0 60.3 %scatter_custom_fusion = s32[257]{0:T(512)S(1)} fusion(s32[16384]{0:T(1024)S(1)} %bitcast.47, s32[16384]{0:T(1024)S(1)} %add_bitcast_fusion, s32[]{:T(128)} %constant.19.clone.1), kind=kCustom, calls=%fused_computation.54 | custom fusion | bytes 1032 | tf_op jit(solution)/shard_map/scatter | solution.py:69
  811.3 1.9 gather_fusion.2
  813.3 8.3 concatenate.11
  821.5 7.8 gather_fusion.3
  829.3 8.3 concatenate.9
  837.6 7.9 gather_fusion
  845.5 3.3 fusion.10
  854.2 2.3 fusion.15
  856.5 2.5 reshape.148
  859.0 6.4 all-to-all-start.1
  865.5 4.4 fusion.18
  869.9 2.5 reshape.145
  872.4 14.2 %all-to-all-done.1 = bf16[128,2,2048]{2,1,0:T(2,128)(2,1)} async-done(((bf16[128,2,2048]{2,1,0:T(2,128)(2,1)}), bf16[128,2,2048]{2,1,0:T(2,128)(2,1)}, u32[]{:S(2)}, u32[]{:S(2)}) %all-to-all-start.1) | async-done | bytes 1048608 | tf_op jit(solution)/shard_map/all_to_all | solution.py:85
  886.6 7.7 all-to-all-start
  895.2 2.3 reshape.149
  897.4 3.6 gather_fusion.4
  901.0 2.0 bitcast_reduce_fusion
  903.0 12.6 %all-to-all-done = bf16[128,2,2048]{2,1,0:T(2,128)(2,1)} async-done(((bf16[128,2,2048]{2,1,0:T(2,128)(2,1)}), bf16[128,2,2048]{2,1,0:T(2,128)(2,1)}, u32[]{:S(2)}, u32[]{:S(2)}) %all-to-all-start) | async-done | bytes 1048608 | tf_op jit(solution)/shard_map/all_to_all | solution.py:78
  915.6 2.2 reshape.146
  917.8 3.6 gather_fusion.1
  922.7 2.1 fusion.21
  (60 shorter events, 16.3 us)
Async XLA Ops:
  7.2 841.6 %copy-start = (bf16[1,2048,768]{2,1,0:T(8,128)(2,1)S(1)}, bf16[1,2048,768]{2,1,0:T(8,128)(2,1)}, u32[]{:S(2)}) copy-start(bf16[1,2048,768]{2,1,0:T(8,128)(2,1)} %param.11) | copy-start | bytes 9437188
  7.2 372.3 %copy-start.5 = (f32[16,8]{0,1:T(8,128)S(1)}, f32[16,8]{0,1:T(8,128)}, u32[]{:S(2)}) copy-start(f32[16,8]{0,1:T(8,128)} %param.9) | copy-start | bytes 1540
  7.2 806.1 %all-gather.7.cloned.1.call-start = ((), (), s32[]{:S(2)}) async-start(), calls=%async_computation.3 | async-start | bytes 8454144 | tf_op jit(solution)/shard_map/all_gather | solution.py:57
  7.9 821.4 %all-gather.5.cloned.1.call-start = ((), (), s32[]{:S(2)}) async-start(), calls=%async_computation.2 | async-start | bytes 8454144 | tf_op jit(solution)/shard_map/all_gather | solution.py:56
  845.5 3.3 copy-start.2
  848.8 4.6 copy-start.8
  848.8 1.5 copy-start.1
  848.8 2.5 copy-start.7
  851.3 2.1 copy-start.9
  852.3 1.9 copy-start.6
  859.0 27.5 %all-to-all-start.1 = ((bf16[128,2,2048]{2,1,0:T(2,128)(2,1)}), bf16[128,2,2048]{2,1,0:T(2,128)(2,1)}, u32[]{:S(2)}, u32[]{:S(2)}) async-start(bf16[128,2,2048]{2,1,0:T(2,128)(2,1)} %reshape.148), calls=%async_computation.1 | async-start | bytes 2097152 | tf_op jit(solution)/shard_map/all_to_all | solution.py:85
  869.9 24.4 %copy-start.4 = (s32[16,8]{0,1:T(8,128)S(1)}, s32[16,8]{0,1:T(8,128)}, u32[]{:S(2)}) copy-start(s32[16,8]{0,1:T(8,128)} %param.8) | copy-start | bytes 1540
  886.6 29.0 %all-to-all-start = ((bf16[128,2,2048]{2,1,0:T(2,128)(2,1)}), bf16[128,2,2048]{2,1,0:T(2,128)(2,1)}, u32[]{:S(2)}, u32[]{:S(2)}) async-start(bf16[128,2,2048]{2,1,0:T(2,128)(2,1)} %reshape.145), calls=%async_computation | async-start | bytes 2097152 | tf_op jit(solution)/shard_map/all_to_all | solution.py:78
  903.0 18.4 %copy-start.3 = (bf16[16,2048]{1,0:T(8,128)(2,1)S(1)}, bf16[16,2048]{1,0:T(8,128)(2,1)}, u32[]{:S(2)}) copy-start(bf16[16,2048]{1,0:T(8,128)(2,1)} %param.13) | copy-start | bytes 196612
Sparse Core Ops, SparseCore 0:
  11.6 126.3 all-gather.6
  141.6 121.2 all-gather.4
where the time goes:
time: 933 us; the launch traced here: 932 us
  blocking collectives  733 us (79%)
  local copies, waits for them, and re-layouts  123 us (13%)
  waiting for transfers between devices  28.1 us (3%)
  between operations  14.3 us (2%)
  starting transfers between devices  14.2 us (2%)
  matrix products  12.9 us (1%)
    all_gather x1, blocking collectives, local(): all_gates = lax.all_gather(gate_values, 'expert', axis=0, tiled=True)  367 us
    all_gather x1, blocking collectives, local(): gathered_ids = lax.all_gather(expert_ids, 'expert', axis=0, tiled=True)  366 us
    scatter x1, local copies, waits for them, and re-layouts, local(): slot_table = jnp.full((slot_total + 1,), experts * entry_count, jnp.int32...  60.3 us
  transfers between devices with their start and end apart: 4, of which 2 were waited for; matrix products, arithmetic and copies ran while one was open for 11% of the time, Pallas kernels for 0%

commit v1 on v0

v1 whole, which is shorter than its diff:
```python
import jax
import jax.numpy as jnp
from jax import lax
from jax.sharding import PartitionSpec as P


def expert_forward(inputs, gate_matrix, up_matrix, down_matrix):
    pre_gate = jnp.dot(inputs, gate_matrix, preferred_element_type=jnp.float32)
    pre_up = jnp.dot(inputs, up_matrix, preferred_element_type=jnp.float32)
    hidden = (pre_gate * jax.nn.sigmoid(pre_gate) * pre_up).astype(jnp.bfloat16)
    output = jnp.dot(hidden, down_matrix, preferred_element_type=jnp.float32).astype(jnp.bfloat16)
    return (output, pre_gate, pre_up)


def expert_backward(grad_output, pre_gate, pre_up, gate_matrix, up_matrix, down_matrix):
    contract = (((1,), (1,)), ((), ()))
    grad_hidden = lax.dot_general(
        grad_output, down_matrix, contract, preferred_element_type=jnp.float32
    )
    sigmoid = jax.nn.sigmoid(pre_gate)
    grad_gate = (grad_hidden * pre_up * sigmoid * (1.0 + pre_gate * (1.0 - sigmoid))).astype(
        jnp.bfloat16
    )
    grad_up = (grad_hidden * pre_gate * sigmoid).astype(jnp.bfloat16)
    first_part = lax.dot_general(
        grad_gate, gate_matrix, contract, preferred_element_type=jnp.float32
    )
    second_part = lax.dot_general(grad_up, up_matrix, contract, preferred_element_type=jnp.float32)
    return (first_part + second_part).astype(jnp.bfloat16)


def split_three(values):
    high = lax.reduce_precision(values, 8, 7)
    rest = values - high
    middle = lax.reduce_precision(rest, 8, 7)
    low = lax.reduce_precision(rest - middle, 8, 7)
    return high, middle, low


def exchange(rows, experts, capacity):
    width = rows.shape[1]
    return lax.all_to_all(
        rows.reshape(experts, capacity, width), "expert", split_axis=0, concat_axis=0, tiled=True
    ).reshape(experts * capacity, width)


def local(tokens, expert_ids, gate_values, w_gate, w_up, w_down, cotangent):
    row_count, _ = tokens.shape
    top_count = expert_ids.shape[1]
    experts = lax.axis_size("expert")
    capacity = 2
    slot_total = experts * capacity
    entry_count = row_count * top_count
    gate_matrix = w_gate[0]
    up_matrix = w_up[0]
    down_matrix = w_down[0]
    ids = expert_ids.T.reshape(-1)
    gates = gate_values.T.reshape(-1)
    order = jnp.arange(entry_count, dtype=jnp.int32)
    earlier = (ids[:, None] == ids[None, :]) & (order[:, None] < order[None, :])
    ranked = jnp.sum(earlier.astype(jnp.int32), axis=0)
    places = ids * capacity + ranked
    slots = jnp.arange(slot_total, dtype=jnp.int32)
    hit = slots[:, None] == places[None, :]
    hit_by = hit.reshape(slot_total, top_count, row_count)
    select = jnp.any(hit_by, axis=1).astype(jnp.bfloat16)
    slot_gates = jnp.sum(jnp.where(hit, gates[None, :], 0.0), axis=1)
    weights = jnp.sum(
        jnp.where(hit_by, gates.reshape(1, top_count, row_count), 0.0), axis=1
    )
    sent_rows = jnp.dot(select, tokens, preferred_element_type=jnp.float32).astype(jnp.bfloat16)
    sent_grads = (
        slot_gates[:, None] * jnp.dot(select, cotangent, preferred_element_type=jnp.float32)
    ).astype(jnp.bfloat16)
    received = exchange(sent_rows, experts, capacity)
    incoming = exchange(sent_grads, experts, capacity)
    output, pre_gate, pre_up = expert_forward(received, gate_matrix, up_matrix, down_matrix)
    returned = exchange(output, experts, capacity)
    grad_rows = expert_backward(incoming, pre_gate, pre_up, gate_matrix, up_matrix, down_matrix)
    returned_grads = exchange(grad_rows, experts, capacity)
    over_slots = (((0,), (0,)), ((), ()))
    parts = jnp.concatenate([part.astype(jnp.bfloat16) for part in split_three(weights)], axis=1)
    mixed = lax.dot_general(parts, returned, over_slots, preferred_element_type=jnp.float32)
    mixed = mixed.reshape(3, row_count, -1)
    mixed_rows = (mixed[2] + mixed[1] + mixed[0]).astype(jnp.bfloat16)
    scores = lax.dot_general(
        cotangent, returned, (((1,), (1,)), ((), ())), preferred_element_type=jnp.float32
    )
    picked = jnp.where(hit_by, scores.T[:, None, :], 0.0)
    gate_grads = jnp.sum(picked, axis=0).T
    row_grads = lax.dot_general(
        select, returned_grads, over_slots, preferred_element_type=jnp.float32
    ).astype(jnp.bfloat16)
    return (mixed_rows, row_grads, gate_grads)


def solution(mesh):
    return jax.shard_map(
        local,
        mesh=mesh,
        in_specs=(
            P(("dp", "expert"), None),
            P(("dp", "expert"), None),
            P(("dp", "expert"), None),
            P("expert", None, None),
            P("expert", None, None),
            P("expert", None, None),
            P(("dp", "expert"), None),
        ),
        out_specs=(P(("dp", "expert"), None), P(("dp", "expert"), None), P(("dp", "expert"), None)),
        check_vma=False,
    )
```

time: 933 us -> 165 us (0.18)
  blocking collectives: 733 us -> 0 us
  local copies, waits for them, and re-layouts: 123 us -> 22.3 us
  waiting for transfers between devices: 28.1 us -> 79.5 us
  starting transfers between devices: 14.2 us -> 38.6 us
  between operations: 14.3 us -> 0.82 us
    all_gather x2 -> x0, blocking collectives: 733 us -> none  [the longest x1 367 us: local(): all_gates = lax.all_gather(gate_values, 'expert', axis=0, tiled=True)]
    scatter x1 -> x0, local copies, waits for them, and re-layouts: 60.3 us -> none  [local(): slot_table = jnp.full((slot_total + 1,), experts * entry_count, jnp.int32...]
    all_to_all x2 -> x4, waiting for transfers between devices: 26.7 us -> 79.5 us  [exchange(): lax.all_to_all(rows.reshape(experts, capacity, width), 'expert', split_ax...]
    gather x5 -> x0, local copies, waits for them, and re-layouts: 24.8 us -> none  [the longest x1 7.89 us: local(): received = jnp.concatenate([all_tokens, padding], axis=0)[token_of]]
    all_to_all x2 -> x4, starting transfers between devices: 14.1 us -> 38.6 us  [exchange(): lax.all_to_all(rows.reshape(experts, capacity, width), 'expert', split_ax...]
    concatenate x2 -> x0, local copies, waits for them, and re-layouts: 16.6 us -> none  [the longest x1 8.28 us: local(): chosen = jnp.concatenate([all_cotangent, padding], axis=0)[token_of]]
    reshape x6 -> x8, local copies, waits for them, and re-layouts: 11.3 us -> 19.1 us  [the longest x4 10.1 us: exchange(): rows.reshape(experts, capacity, width)]
  transfers between devices with their start and end apart: 4 -> 4, of which waited for: 2 -> 4; matrix products, arithmetic and copies ran while one was open for 11% -> 20% of each run, Pallas kernels for 0% -> 0%
where the time goes in v1:
time: 165 us; the launch traced here: 164 us
  waiting for transfers between devices  79.5 us (48%)
  starting transfers between devices  38.6 us (23%)
  local copies, waits for them, and re-layouts  22.3 us (14%)
  matrix products  20.8 us (13%)
  other arithmetic  2.45 us (1%)
    all_to_all x4, waiting for transfers between devices, exchange(): lax.all_to_all(rows.reshape(experts, capacity, width), 'expert', split_ax...  79.5 us
    all_to_all x4, starting transfers between devices, exchange(): lax.all_to_all(rows.reshape(experts, capacity, width), 'expert', split_ax...  38.6 us
    reshape x4, local copies, waits for them, and re-layouts, exchange(): rows.reshape(experts, capacity, width)  10.1 us
    reshape x4, local copies, waits for them, and re-layouts, exchange(): return lax.all_to_all(rows.reshape(experts, capacity, width), 'expert', s...  8.99 us
    dot_general x1, matrix products, expert_forward(): pre_gate = jnp.dot(inputs, gate_matrix, preferred_element_type=jnp.float32)  3.32 us
  transfers between devices with their start and end apart: 4, of which 4 were waited for; matrix products, arithmetic and copies ran while one was open for 20% of the time, Pallas kernels for 0%

profile of v1, /device:TPU:32, one launch (start us, length us, event | category | flops | bytes accessed | tf_op | source)
XLA Modules:
  0.0 164.3 jit_solution(11274077211523963759)
XLA Ops:
  2.6 2.3 %convolution_convert_fusion = bf16[256,2048]{1,0:T(8,128)(2,1)} fusion(pred[256,16]{0,1:T(8,128)(4,1)S(1)} %fusion.26, bf16[16,2048]{1,0:T(8,128)(2,1)} %param.7), kind=kOutput, calls=%fused_computation.15 | convolution fusion | flops 17301504 | bytes 1118208 | tf_op jit(solution)/shard_map/dot_general | solution.py:71
  4.8 2.5 %reshape.62 = bf16[128,2,2048]{2,1,0:T(2,128)(2,1)} reshape(bf16[256,2048]{1,0:T(8,128)(2,1)} %convolution_convert_fusion) | data formatting | bytes 2097152 | tf_op jit(solution)/shard_map/reshape | solution.py:43
  7.4 15.5 %all-to-all-start = ((bf16[128,2,2048]{2,1,0:T(2,128)(2,1)}), bf16[128,2,2048]{2,1,0:T(2,128)(2,1)}, u32[]{:S(2)}, u32[]{:S(2)}) async-start(bf16[128,2,2048]{2,1,0:T(2,128)(2,1)} %reshape.62), calls=%async_computation | async-start | bytes 2097152 | tf_op jit(solution)/shard_map/all_to_all | solution.py:42
  24.5 2.5 %reshape.66 = bf16[128,2,2048]{2,1,0:T(2,128)(2,1)} reshape(bf16[256,2048]{1,0:T(8,128)(2,1)} %fusion.18) | data formatting | bytes 2097152 | tf_op jit(solution)/shard_map/reshape | solution.py:43
  27.1 26.8 %all-to-all-done = bf16[128,2,2048]{2,1,0:T(2,128)(2,1)} async-done(((bf16[128,2,2048]{2,1,0:T(2,128)(2,1)}), bf16[128,2,2048]{2,1,0:T(2,128)(2,1)}, u32[]{:S(2)}, u32[]{:S(2)}) %all-to-all-start) | async-done | bytes 1048608 | tf_op jit(solution)/shard_map/all_to_all | solution.py:42
  53.9 7.7 %all-to-all-start.2 = ((bf16[128,2,2048]{2,1,0:T(2,128)(2,1)}), bf16[128,2,2048]{2,1,0:T(2,128)(2,1)}, u32[]{:S(2)}, u32[]{:S(2)}) async-start(bf16[128,2,2048]{2,1,0:T(2,128)(2,1)} %reshape.66), calls=%async_computation.2 | async-start | bytes 2097152 | tf_op jit(solution)/shard_map/all_to_all | solution.py:42
  61.6 2.2 %reshape.63 = bf16[256,2048]{1,0:T(8,128)(2,1)} reshape(bf16[128,2,2048]{2,1,0:T(2,128)(2,1)} %all-to-all-done) | data formatting | bytes 2097152 | tf_op jit(solution)/shard_map/reshape | solution.py:44
  63.8 3.3 %fusion.10 = f32[256,768]{1,0:T(8,128)S(1)} fusion(bf16[256,2048]{1,0:T(8,128)(2,1)} %reshape.63, bf16[1,2048,768]{2,1,0:T(8,128)(2,1)} %param.10), kind=kOutput, calls=%fused_computation.10 | convolution fusion | flops 805306368 | bytes 4980736 | tf_op jit(solution)/shard_map/dot_general | solution.py:8
  69.2 2.0 %fusion.19 = bf16[256,2048]{1,0:T(8,128)(2,1)} fusion(bf16[1,768,2048]{2,1,0:T(8,128)(2,1)S(1)} %copy-done, f32[256,768]{1,0:T(8,128)S(1)} %fusion.6, f32[256,768]{1,0:T(8,128)S(1)} %fusion.10), kind=kOutput, calls=%fused_computation.17 | convolution fusion | flops 807010304 | bytes 5767168 | tf_op jit(solution)/shard_map/dot_general | solution.py:11
  71.2 2.5 %reshape.64 = bf16[128,2,2048]{2,1,0:T(2,128)(2,1)} reshape(bf16[256,2048]{1,0:T(8,128)(2,1)} %fusion.19) | data formatting | bytes 2097152 | tf_op jit(solution)/shard_map/reshape | solution.py:43
  73.7 17.3 %all-to-all-done.2 = bf16[128,2,2048]{2,1,0:T(2,128)(2,1)} async-done(((bf16[128,2,2048]{2,1,0:T(2,128)(2,1)}), bf16[128,2,2048]{2,1,0:T(2,128)(2,1)}, u32[]{:S(2)}, u32[]{:S(2)}) %all-to-all-start.2) | async-done | bytes 1048608 | tf_op jit(solution)/shard_map/all_to_all | solution.py:42
  91.1 7.7 %all-to-all-start.1 = ((bf16[128,2,2048]{2,1,0:T(2,128)(2,1)}), bf16[128,2,2048]{2,1,0:T(2,128)(2,1)}, u32[]{:S(2)}, u32[]{:S(2)}) async-start(bf16[128,2,2048]{2,1,0:T(2,128)(2,1)} %reshape.64), calls=%async_computation.1 | async-start | bytes 2097152 | tf_op jit(solution)/shard_map/all_to_all | solution.py:42
  98.8 2.2 %reshape.67 = bf16[256,2048]{1,0:T(8,128)(2,1)} reshape(bf16[128,2,2048]{2,1,0:T(2,128)(2,1)} %all-to-all-done.2) | data formatting | bytes 2097152 | tf_op jit(solution)/shard_map/reshape | solution.py:44
  101.0 2.4 %fusion = f32[256,768]{1,0:T(8,128)S(1)} fusion(bf16[256,2048]{1,0:T(8,128)(2,1)} %reshape.67, bf16[1,768,2048]{2,1,0:T(8,128)(2,1)S(1)} %copy-done), kind=kOutput, calls=%fused_computation | convolution fusion | flops 805306368 | bytes 4980736 | tf_op jit(solution)/shard_map/dot_general | solution.py:17
  105.5 2.1 %fusion.15 = bf16[256,2048]{1,0:T(8,128)(2,1)} fusion(f32[256,2048]{1,0:T(8,128)S(1)} %fusion.4, bf16[1,2048,768]{2,1,0:T(8,128)(2,1)S(1)} %copy-done.6, f32[256,768]{1,0:T(8,128)S(1)} %copy-done.8, f32[256,768]{1,0:T(8,128)S(1)} %fusion, f32[256,768]{1,0:T(8,128)S(1)} %copy-done.10), kind=kOutput, calls=%fused_computation.14 | convolution fusion | flops 808321024 | bytes 8650752 | tf_op jit(solution)/shard_map/dot_general | solution.py:25
  107.6 2.5 %reshape.68 = bf16[128,2,2048]{2,1,0:T(2,128)(2,1)} reshape(bf16[256,2048]{1,0:T(8,128)(2,1)} %fusion.15) | data formatting | bytes 2097152 | tf_op jit(solution)/shard_map/reshape | solution.py:43
  110.2 16.4 %all-to-all-done.1 = bf16[128,2,2048]{2,1,0:T(2,128)(2,1)} async-done(((bf16[128,2,2048]{2,1,0:T(2,128)(2,1)}), bf16[128,2,2048]{2,1,0:T(2,128)(2,1)}, u32[]{:S(2)}, u32[]{:S(2)}) %all-to-all-start.1) | async-done | bytes 1048608 | tf_op jit(solution)/shard_map/all_to_all | solution.py:42
  126.5 7.7 %all-to-all-start.3 = ((bf16[128,2,2048]{2,1,0:T(2,128)(2,1)}), bf16[128,2,2048]{2,1,0:T(2,128)(2,1)}, u32[]{:S(2)}, u32[]{:S(2)}) async-start(bf16[128,2,2048]{2,1,0:T(2,128)(2,1)} %reshape.68), calls=%async_computation.3 | async-start | bytes 2097152 | tf_op jit(solution)/shard_map/all_to_all | solution.py:42
  134.2 2.2 %reshape.65 = bf16[256,2048]{1,0:T(8,128)(2,1)} reshape(bf16[128,2,2048]{2,1,0:T(2,128)(2,1)} %all-to-all-done.1) | data formatting | bytes 2097152 | tf_op jit(solution)/shard_map/reshape | solution.py:44
  136.5 1.6 fusion.40
  138.9 1.5 fusion.28
  141.0 18.9 %all-to-all-done.3 = bf16[128,2,2048]{2,1,0:T(2,128)(2,1)} async-done(((bf16[128,2,2048]{2,1,0:T(2,128)(2,1)}), bf16[128,2,2048]{2,1,0:T(2,128)(2,1)}, u32[]{:S(2)}, u32[]{:S(2)}) %all-to-all-start.3) | async-done | bytes 1048608 | tf_op jit(solution)/shard_map/all_to_all | solution.py:42
  160.0 2.2 %reshape.69 = bf16[256,2048]{1,0:T(8,128)(2,1)} reshape(bf16[128,2,2048]{2,1,0:T(2,128)(2,1)} %all-to-all-done.3) | data formatting | bytes 2097152 | tf_op jit(solution)/shard_map/reshape | solution.py:44
  162.2 2.1 %convolution_convert_fusion.1 = bf16[16,2048]{1,0:T(8,128)(2,1)} fusion(pred[256,16]{0,1:T(8,128)(4,1)S(1)} %fusion.26, bf16[256,2048]{1,0:T(8,128)(2,1)} %reshape.69), kind=kOutput, calls=%fused_computation.18 | convolution fusion | flops 16809984 | bytes 1118208 | tf_op jit(solution)/shard_map/dot_general | solution.py:91
  (36 shorter events, 9.1 us)
Async XLA Ops:
  0.6 68.5 %copy-start = (bf16[1,768,2048]{2,1,0:T(8,128)(2,1)S(1)}, bf16[1,768,2048]{2,1,0:T(8,128)(2,1)}, u32[]{:S(2)}) copy-start(bf16[1,768,2048]{2,1,0:T(8,128)(2,1)} %param.12) | copy-start | bytes 9437188
  0.6 22.2 %copy-start.3 = (f32[16,8]{0,1:T(8,128)S(1)}, f32[16,8]{0,1:T(8,128)}, u32[]{:S(2)}) copy-start(f32[16,8]{0,1:T(8,128)} %param.9) | copy-start | bytes 1540
  0.7 22.4 %copy-start.2 = (bf16[16,2048]{1,0:T(8,128)(2,1)S(1)}, bf16[16,2048]{1,0:T(8,128)(2,1)}, u32[]{:S(2)}) copy-start(bf16[16,2048]{1,0:T(8,128)(2,1)} %param.13) | copy-start | bytes 196612
  7.4 46.5 %all-to-all-start = ((bf16[128,2,2048]{2,1,0:T(2,128)(2,1)}), bf16[128,2,2048]{2,1,0:T(2,128)(2,1)}, u32[]{:S(2)}, u32[]{:S(2)}) async-start(bf16[128,2,2048]{2,1,0:T(2,128)(2,1)} %reshape.62), calls=%async_computation | async-start | bytes 2097152 | tf_op jit(solution)/shard_map/all_to_all | solution.py:42
  53.9 37.2 %all-to-all-start.2 = ((bf16[128,2,2048]{2,1,0:T(2,128)(2,1)}), bf16[128,2,2048]{2,1,0:T(2,128)(2,1)}, u32[]{:S(2)}, u32[]{:S(2)}) async-start(bf16[128,2,2048]{2,1,0:T(2,128)(2,1)} %reshape.66), calls=%async_computation.2 | async-start | bytes 2097152 | tf_op jit(solution)/shard_map/all_to_all | solution.py:42
  63.8 3.3 %copy-start.1 = (bf16[256,2048]{1,0:T(8,128)(2,1)S(1)}, bf16[256,2048]{1,0:T(8,128)(2,1)}, u32[]{:S(2)}) copy-start(bf16[256,2048]{1,0:T(8,128)(2,1)} %reshape.63) | copy-start | bytes 3145732
  63.8 3.5 %copy-start.4 = (bf16[1,2048,768]{2,1,0:T(8,128)(2,1)S(1)}, bf16[1,2048,768]{2,1,0:T(8,128)(2,1)}, u32[]{:S(2)}) copy-start(bf16[1,2048,768]{2,1,0:T(8,128)(2,1)} %param.11) | copy-start | bytes 9437188
  67.3 1.0 copy-start.7
  68.3 0.9 copy-start.9
  91.1 35.5 %all-to-all-start.1 = ((bf16[128,2,2048]{2,1,0:T(2,128)(2,1)}), bf16[128,2,2048]{2,1,0:T(2,128)(2,1)}, u32[]{:S(2)}, u32[]{:S(2)}) async-start(bf16[128,2,2048]{2,1,0:T(2,128)(2,1)} %reshape.64), calls=%async_computation.1 | async-start | bytes 2097152 | tf_op jit(solution)/shard_map/all_to_all | solution.py:42
  101.0 2.4 %copy-start.5 = (bf16[1,2048,768]{2,1,0:T(8,128)(2,1)S(1)}, bf16[1,2048,768]{2,1,0:T(8,128)(2,1)}, u32[]{:S(2)}) copy-start(bf16[1,2048,768]{2,1,0:T(8,128)(2,1)} %param.11) | copy-start | bytes 9437188
  101.0 2.4 %copy-start.8 = (f32[256,768]{1,0:T(8,128)S(1)}, f32[256,768]{1,0:T(8,128)}, u32[]{:S(2)}) copy-start(f32[256,768]{1,0:T(8,128)} %copy-done.7) | copy-start | bytes 2359300
  103.5 1.9 %copy-start.6 = (bf16[1,2048,768]{2,1,0:T(8,128)(2,1)S(1)}, bf16[1,2048,768]{2,1,0:T(8,128)(2,1)}, u32[]{:S(2)}) copy-start(bf16[1,2048,768]{2,1,0:T(8,128)(2,1)} %param.10) | copy-start | bytes 9437188
  103.5 2.1 %copy-start.10 = (f32[256,768]{1,0:T(8,128)S(1)}, f32[256,768]{1,0:T(8,128)}, u32[]{:S(2)}) copy-start(f32[256,768]{1,0:T(8,128)} %copy-done.9) | copy-start | bytes 2359300
  126.5 33.4 %all-to-all-start.3 = ((bf16[128,2,2048]{2,1,0:T(2,128)(2,1)}), bf16[128,2,2048]{2,1,0:T(2,128)(2,1)}, u32[]{:S(2)}, u32[]{:S(2)}) async-start(bf16[128,2,2048]{2,1,0:T(2,128)(2,1)} %reshape.68), calls=%async_computation.3 | async-start | bytes 2097152 | tf_op jit(solution)/shard_map/all_to_all | solution.py:42

commit v2 on v1

v2 whole, which is shorter than its diff:
```python
import jax
import jax.numpy as jnp
from jax import lax
from jax.experimental import pallas as pl
from jax.experimental.pallas import tpu as pltpu
from jax.sharding import PartitionSpec as P

DEPTH = 8
PLANE = 16
CAPACITY = 2
PLANE_STEP = 15
DEPTH_STEP = 3
ROWS = 16
TOP = 8
WIDTH = 2048
HIDDEN = 768
NOTES = 128
LINE = DEPTH * ROWS
EACH = DEPTH * CAPACITY
SLOTS = PLANE * EACH
BF = jnp.bfloat16
F32 = jnp.float32
COLUMNS = 512
MIB = 1024 * 1024


def iota(shape, dim):
    return lax.broadcasted_iota(jnp.int32, shape, dim)


def parts_of(values):
    high = values.astype(BF)
    rest = values - high.astype(F32)
    middle = rest.astype(BF)
    low = (rest - middle.astype(F32)).astype(BF)
    return high, middle, low


def pack_kernel(tokens_ref, cotangent_ref, ids_ref, gates_ref, out_ref):
    high, middle, low = parts_of(gates_ref[...])
    columns = jnp.concatenate(
        [ids_ref[...].astype(F32), high.astype(F32), middle.astype(F32), low.astype(F32)], axis=0
    )
    columns = jnp.concatenate([columns, jnp.zeros((NOTES - 4 * TOP, ROWS), F32)], axis=0)
    notes = columns.T.astype(BF)
    for start in range(0, LINE, ROWS):
        out_ref[start : start + ROWS, :WIDTH] = tokens_ref[...]
        out_ref[start : start + ROWS, WIDTH : 2 * WIDTH] = cotangent_ref[...]
        out_ref[start : start + ROWS, 2 * WIDTH :] = notes


def tables(depth, notes):
    notes = notes.astype(F32)
    lane = iota((LINE, SLOTS), 1)
    row = iota((LINE, SLOTS), 0)
    named = ((lane // EACH * PLANE_STEP % PLANE) * DEPTH + depth).astype(F32)
    matches = []
    weight = jnp.zeros((LINE, SLOTS), F32)
    member = jnp.zeros((LINE, SLOTS), F32)
    for k in range(TOP):
        match = notes[:, k : k + 1] == named
        gate = (
            notes[:, TOP + k : TOP + k + 1]
            + notes[:, 2 * TOP + k : 2 * TOP + k + 1]
            + notes[:, 3 * TOP + k : 3 * TOP + k + 1]
        )
        weight = jnp.where(match, gate, weight)
        member = jnp.where(match, 1.0, member)
        matches.append(match)
    left = iota((LINE, LINE), 0)
    right = iota((LINE, LINE), 1)
    ahead = ((left // ROWS == right // ROWS) & (right < left)).astype(F32).astype(BF)
    ranked = jnp.dot(ahead, member.astype(BF), preferred_element_type=F32)
    here = (row // ROWS == (lane % EACH) // CAPACITY) & (
        ranked == (lane % CAPACITY).astype(F32)
    )
    hit = jnp.where(here, member, 0.0)
    return hit, hit * weight, matches


def dispatch_kernel(depth_ref, line_ref, out_ref):
    notes = line_ref[:, 2 * WIDTH :]
    hit, weight, _ = tables(depth_ref[0], notes)
    select = hit.T.astype(BF)
    gates = jnp.sum(weight.T, axis=1, keepdims=True)
    for start in range(0, WIDTH, COLUMNS):
        block = line_ref[:, start : start + COLUMNS]
        out_ref[:, start : start + COLUMNS] = jnp.dot(
            select, block, preferred_element_type=F32
        ).astype(BF)
    for start in range(WIDTH, 2 * WIDTH, COLUMNS):
        block = line_ref[:, start : start + COLUMNS]
        out_ref[:, start : start + COLUMNS] = (
            gates * jnp.dot(select, block, preferred_element_type=F32)
        ).astype(BF)


def dot_t(left, right):
    return lax.dot_general(left, right, (((1,), (1,)), ((), ())), preferred_element_type=F32)


def expert_kernel(rows, gate_hbm, up_hbm, down_hbm, out, gate, up, down, sems):
    copies = [
        pltpu.make_async_copy(gate_hbm, gate, sems.at[0]),
        pltpu.make_async_copy(up_hbm, up, sems.at[1]),
        pltpu.make_async_copy(down_hbm, down, sems.at[2]),
    ]
    for copy in copies:
        copy.start()
    inputs = rows[:, :WIDTH]
    copies[0].wait()
    pre_gate = jnp.dot(inputs, gate[...], preferred_element_type=F32)
    copies[1].wait()
    pre_up = jnp.dot(inputs, up[...], preferred_element_type=F32)
    sigmoid = jax.nn.sigmoid(pre_gate)
    hidden = (pre_gate * sigmoid * pre_up).astype(BF)
    copies[2].wait()
    out[:, :WIDTH] = jnp.dot(hidden, down[...], preferred_element_type=F32).astype(BF)
    grad_hidden = dot_t(rows[:, WIDTH:], down[...])
    grad_gate = (grad_hidden * pre_up * sigmoid * (1.0 + pre_gate * (1.0 - sigmoid))).astype(BF)
    grad_up = (grad_hidden * pre_gate * sigmoid).astype(BF)
    out[:, WIDTH:] = (dot_t(grad_gate, gate[...]) + dot_t(grad_up, up[...])).astype(BF)


def combine_kernel(depth_ref, line_ref, back_ref, out_ref):
    hit, weight, matches = tables(depth_ref[0], line_ref[:, 2 * WIDTH :])
    select = hit.astype(BF)
    high, middle, low = parts_of(weight)
    scores = jnp.zeros((LINE, SLOTS), F32)
    for start in range(0, WIDTH, COLUMNS):
        block = back_ref[:, start : start + COLUMNS]
        mixed = (
            jnp.dot(low, block, preferred_element_type=F32)
            + jnp.dot(middle, block, preferred_element_type=F32)
            + jnp.dot(high, block, preferred_element_type=F32)
        )
        out_ref[:, start : start + COLUMNS] = mixed.astype(BF)
        scores = scores + dot_t(line_ref[:, WIDTH + start : WIDTH + start + COLUMNS], block)
    for start in range(WIDTH, 2 * WIDTH, COLUMNS):
        block = back_ref[:, start : start + COLUMNS]
        out_ref[:, start : start + COLUMNS] = jnp.dot(
            select, block, preferred_element_type=F32
        ).astype(BF)
    scores = jnp.where(hit > 0.0, scores, 0.0)
    lane = iota((LINE, NOTES), 1)
    notes = jnp.zeros((LINE, NOTES), F32)
    for k in range(TOP):
        total = jnp.sum(jnp.where(matches[k], scores, 0.0), axis=1, keepdims=True)
        for part, value in enumerate(parts_of(total)):
            notes = jnp.where(lane == part * TOP + k, value.astype(F32), notes)
    out_ref[:, 2 * WIDTH :] = notes.astype(BF)


def finish_kernel(parts_ref, mixed_ref, rows_ref, gates_ref):
    def total(start, stop):
        value = parts_ref[0, :, start:stop].astype(F32)
        for place in range(1, DEPTH):
            value = value + parts_ref[place, :, start:stop].astype(F32)
        return value

    mixed_ref[...] = total(0, WIDTH).astype(BF)
    rows_ref[...] = total(WIDTH, 2 * WIDTH).astype(BF)
    columns = total(2 * WIDTH, 2 * WIDTH + NOTES).T
    gates_ref[...] = columns[:TOP] + columns[TOP : 2 * TOP] + columns[2 * TOP : 3 * TOP]


def local(tokens, expert_ids, gate_values, w_gate, w_up, w_down, cotangent):
    total = 2 * WIDTH + NOTES
    place = lax.axis_index("expert")
    depth = (place % DEPTH).astype(jnp.int32).reshape(1)
    spots = [PLANE_STEP * spot % PLANE for spot in range(PLANE)]
    levels = [DEPTH_STEP * level % DEPTH for level in range(DEPTH)]
    planes = [[spot * DEPTH + level for spot in spots] for level in range(DEPTH)]
    lines = [[spot * DEPTH + level for level in levels] for spot in range(PLANE)]

    def exchange(blocks, groups):
        return lax.all_to_all(
            blocks, "expert", split_axis=0, concat_axis=0, tiled=True, axis_index_groups=groups
        )

    def near(array):
        return pltpu.with_memory_space_constraint(array, pltpu.VMEM)

    vmem = pl.BlockSpec(memory_space=pltpu.VMEM)
    smem = pl.BlockSpec(memory_space=pltpu.SMEM)
    anywhere = pl.BlockSpec(memory_space=pl.ANY)
    packed = pl.pallas_call(
        pack_kernel,
        out_shape=pltpu.VMEM((LINE, total), BF),
        in_specs=[vmem] * 4,
        out_specs=vmem,
        name="pack",
        compiler_params=pltpu.CompilerParams(vmem_limit_bytes=8 * MIB),
    )(tokens, cotangent, expert_ids.T, gate_values.T)
    line = near(exchange(packed.reshape(DEPTH, ROWS, total), lines).reshape(LINE, total))
    sent = pl.pallas_call(
        dispatch_kernel,
        out_shape=pltpu.VMEM((SLOTS, 2 * WIDTH), BF),
        in_specs=[smem, vmem],
        out_specs=vmem,
        name="dispatch",
        compiler_params=pltpu.CompilerParams(vmem_limit_bytes=16 * MIB),
    )(depth, line)
    received = exchange(sent.reshape(PLANE, EACH, 2 * WIDTH), planes)
    received = near(received.reshape(SLOTS, 2 * WIDTH))
    output = pl.pallas_call(
        expert_kernel,
        out_shape=pltpu.VMEM((SLOTS, 2 * WIDTH), BF),
        in_specs=[vmem, anywhere, anywhere, anywhere],
        out_specs=vmem,
        scratch_shapes=[
            pltpu.VMEM((WIDTH, HIDDEN), BF),
            pltpu.VMEM((WIDTH, HIDDEN), BF),
            pltpu.VMEM((HIDDEN, WIDTH), BF),
            pltpu.SemaphoreType.DMA((3,)),
        ],
        name="expert",
        compiler_params=pltpu.CompilerParams(vmem_limit_bytes=28 * MIB),
    )(received, w_gate[0], w_up[0], w_down[0])
    back = exchange(output.reshape(PLANE, EACH, 2 * WIDTH), planes)
    back = near(back.reshape(SLOTS, 2 * WIDTH))
    parts = pl.pallas_call(
        combine_kernel,
        out_shape=pltpu.VMEM((LINE, total), BF),
        in_specs=[smem, vmem, vmem],
        out_specs=vmem,
        name="combine",
        compiler_params=pltpu.CompilerParams(vmem_limit_bytes=16 * MIB),
    )(depth, line, back)
    parts = near(exchange(parts.reshape(DEPTH, ROWS, total), lines))
    mixed_rows, row_grads, gate_grads = pl.pallas_call(
        finish_kernel,
        out_shape=(
            jax.ShapeDtypeStruct((ROWS, WIDTH), BF),
            jax.ShapeDtypeStruct((ROWS, WIDTH), BF),
            jax.ShapeDtypeStruct((TOP, ROWS), F32),
        ),
        in_specs=[vmem],
        out_specs=(vmem, vmem, vmem),
        name="finish",
        compiler_params=pltpu.CompilerParams(vmem_limit_bytes=8 * MIB),
    )(parts)
    return (mixed_rows, row_grads, gate_grads.T)


def solution(mesh):
    return jax.shard_map(
        local,
        mesh=mesh,
        in_specs=(
            P(("dp", "expert"), None),
            P(("dp", "expert"), None),
            P(("dp", "expert"), None),
            P("expert", None, None),
            P("expert", None, None),
            P("expert", None, None),
            P(("dp", "expert"), None),
        ),
        out_specs=(P(("dp", "expert"), None), P(("dp", "expert"), None), P(("dp", "expert"), None)),
        check_vma=False,
    )
```

time: 165 us -> 148 us (0.90)
  blocking collectives: 0 us -> 93.1 us
  waiting for transfers between devices: 79.5 us -> 28 us
  starting transfers between devices: 38.6 us -> 8.57 us
  matrix products: 20.8 us -> 0 us
  local copies, waits for them, and re-layouts: 22.3 us -> 4.94 us
  Pallas kernels: 0 us -> 12.2 us
  other arithmetic: 2.45 us -> 0 us
    all_to_all x0 -> x3, blocking collectives: none -> 93.1 us  [exchange(): lax.all_to_all(blocks, 'expert', split_axis=0, concat_axis=0, tiled=True,...]
    all_to_all x4 -> x1, waiting for transfers between devices: 79.5 us -> 28 us  [exchange(): lax.all_to_all(blocks, 'expert', split_axis=0, concat_axis=0, tiled=True,...]
    all_to_all x4 -> x1, starting transfers between devices: 38.6 us -> 8.57 us  [exchange(): lax.all_to_all(blocks, 'expert', split_axis=0, concat_axis=0, tiled=True,...]
    dot_general x11 -> x0, matrix products: 20.8 us -> none  [the longest x1 3.32 us: expert_forward(): pre_gate = jnp.dot(inputs, gate_matrix, preferred_element_type=jnp.float32)]
    reshape x8 -> x0, local copies, waits for them, and re-layouts: 19.1 us -> none  [the longest x4 10.1 us: exchange(): rows.reshape(experts, capacity, width)]
    pallas_call x0 -> x5, Pallas kernels: none -> 12.2 us  [the longest x1 7.5 us: local(): pl.pallas_call(expert_kernel, out_shape=pltpu.VMEM((SLOTS, 2 * WIDTH), BF...]
    unnamed x22 -> x14, local copies, waits for them, and re-layouts: 2.08 us -> 4.94 us
  transfers between devices with their start and end apart: 4 -> 1, of which waited for: 4 -> 1; matrix products, arithmetic and copies ran while one was open for 20% -> 0% of each run, Pallas kernels for 0% -> 0%
where the time goes in v2:
time: 148 us; the launch traced here: 147 us
  blocking collectives  93.1 us (63%)
  waiting for transfers between devices  28 us (19%)
  Pallas kernels  12.2 us (8%)
  starting transfers between devices  8.57 us (6%)
  local copies, waits for them, and re-layouts  4.94 us (3%)
    all_to_all x3, blocking collectives, exchange(): lax.all_to_all(blocks, 'expert', split_axis=0, concat_axis=0, tiled=True,...  93.1 us
    all_to_all x1, waiting for transfers between devices, exchange(): lax.all_to_all(blocks, 'expert', split_axis=0, concat_axis=0, tiled=True,...  28 us
    all_to_all x1, starting transfers between devices, exchange(): lax.all_to_all(blocks, 'expert', split_axis=0, concat_axis=0, tiled=True,...  8.57 us
    pallas_call x1, Pallas kernels, local(): pl.pallas_call(expert_kernel, out_shape=pltpu.VMEM((SLOTS, 2 * WIDTH), BF...  7.5 us
    unnamed x14, local copies, waits for them, and re-layouts  4.94 us
  transfers between devices with their start and end apart: 1, of which 1 were waited for; matrix products, arithmetic and copies ran while one was open for 0% of the time, Pallas kernels for 0%

profile of v2, /device:TPU:32, one launch (start us, length us, event | category | flops | bytes accessed | tf_op | source)
XLA Modules:
  0.0 147.4 jit_solution(4415217293417992357)
XLA Ops:
  0.6 0.0 copy-start.3
  0.6 0.8 copy-done.3
  1.5 0.0 copy-start.4
  1.5 0.8 copy-done.4
  2.3 0.0 copy-start.5
  2.3 0.7 copy-done.5
  3.0 0.0 copy-start.6
  3.0 0.7 copy-done.6
  3.7 1.1 pack.1
  4.7 8.6 %all-to-all-start = ((bf16[8,16,4224]{2,1,0:T(8,128)(2,1)}), bf16[8,16,4224]{2,1,0:T(8,128)(2,1)S(1)}, u32[]{:S(2)}, u32[]{:S(2)}) async-start(bf16[8,16,4224]{2,1,0:T(8,128)(2,1)} %bitcast.3), calls=%async_computation | async-start | bytes 2162688 | tf_op jit(solution)/shard_map/all_to_all | solution.py:177
  13.3 28.0 %all-to-all-done = bf16[8,16,4224]{2,1,0:T(8,128)(2,1)S(1)} async-done(((bf16[8,16,4224]{2,1,0:T(8,128)(2,1)}), bf16[8,16,4224]{2,1,0:T(8,128)(2,1)S(1)}, u32[]{:S(2)}, u32[]{:S(2)}) %all-to-all-start) | async-done | bytes 1081376 | tf_op jit(solution)/shard_map/all_to_all | solution.py:177
  41.3 0.0 copy-start.1
  41.3 1.1 dispatch.1
  42.4 0.0 copy-start
  42.5 34.4 %all_to_all.20 = bf16[16,16,4096]{2,1,0:T(8,128)(2,1)S(1)} all-to-all(bf16[16,16,4096]{2,1,0:T(8,128)(2,1)S(1)} %bitcast.17), channel_id=1, replica_groups={{0,240,224,208,192,176,160,144,128,112,96,80,64,48,32,16},{2,242,226,21..., dimensions={0} | all-to-all | bytes 4194304 | tf_op jit(solution)/shard_map/all_to_all | solution.py:177
  76.9 0.0 copy-done.1
  76.9 0.0 copy-done
  76.9 0.0 copy-start.2
  76.9 1.9 %copy-done.2 = bf16[1,768,2048]{2,1,0:T(8,128)(2,1)S(1)} copy-done((bf16[1,768,2048]{2,1,0:T(8,128)(2,1)S(1)}, bf16[1,768,2048]{2,1,0:T(8,128)(2,1)}, u32[]{:S(2)}) %copy-start.2) | copy-done | bytes 3145752
  78.8 7.5 %expert.1 = bf16[256,4096]{1,0:T(8,128)(2,1)S(1)} custom-call(bf16[256,4096]{1,0:T(8,128)(2,1)S(1)} %bitcast.18, bf16[2048,768]{1,0:T(8,128)(2,1)S(1)} %bitcast.21, bf16[2048,768]{1,0:T(8,128)(2,1)S(1)} %bitcast.22, bf16[768,2048]{1,0:T(8,128)(2,1)S(1)} %bitcast.23), custom_call_target="tpu_custom_call" | custom-call | tf_op jit(solution)/shard_map/expert/pallas_call | solution.py:206
  86.3 29.4 %all_to_all.21 = bf16[16,16,4096]{2,1,0:T(8,128)(2,1)S(1)} all-to-all(bf16[16,16,4096]{2,1,0:T(8,128)(2,1)S(1)} %bitcast.19), channel_id=1, replica_groups={{0,240,224,208,192,176,160,144,128,112,96,80,64,48,32,16},{2,242,226,21..., dimensions={0} | all-to-all | bytes 4194304 | tf_op jit(solution)/shard_map/all_to_all | solution.py:177
  115.7 1.7 %combine.1 = bf16[128,4224]{1,0:T(8,128)(2,1)S(1)} custom-call(s32[1]{0:T(128)} %bitcast.depth_ref, bf16[128,4224]{1,0:T(8,128)(2,1)S(1)} %bitcast.15, bf16[256,4096]{1,0:T(8,128)(2,1)S(1)} %bitcast.16), custom_call_target="tpu_custom_call" | custom-call | tf_op jit(solution)/shard_map/combine/pallas_call | solution.py:222
  117.4 29.3 %all_to_all.22.parts_ref = bf16[8,16,4224]{2,1,0:T(8,128)(2,1)S(1)} all-to-all(bf16[8,16,4224]{2,1,0:T(8,128)(2,1)S(1)} %bitcast.20), channel_id=1, replica_groups={{0,6,12,2,8,14,4,10},{16,22,28,18,24,30,20,26},{32,38,44,34,40,46,36,42..., dimensions={0} | all-to-all | bytes 2162688 | tf_op jit(solution)/shard_map/all_to_all | solution.py:177
  146.7 0.8 finish.1
Async XLA Ops:
  0.6 0.8 copy-start.3
  1.5 0.8 copy-start.4
  2.3 0.7 copy-start.5
  3.0 0.7 copy-start.6
  4.7 36.5 %all-to-all-start = ((bf16[8,16,4224]{2,1,0:T(8,128)(2,1)}), bf16[8,16,4224]{2,1,0:T(8,128)(2,1)S(1)}, u32[]{:S(2)}, u32[]{:S(2)}) async-start(bf16[8,16,4224]{2,1,0:T(8,128)(2,1)} %bitcast.3), calls=%async_computation | async-start | bytes 2162688 | tf_op jit(solution)/shard_map/all_to_all | solution.py:177
  41.3 35.6 %copy-start.1 = (bf16[1,2048,768]{2,1,0:T(8,128)(2,1)S(1)}, bf16[1,2048,768]{2,1,0:T(8,128)(2,1)}, u32[]{:S(2)}) copy-start(bf16[1,2048,768]{2,1,0:T(8,128)(2,1)} %param.11) | copy-start | bytes 9437188
  42.4 34.5 %copy-start = (bf16[1,2048,768]{2,1,0:T(8,128)(2,1)S(1)}, bf16[1,2048,768]{2,1,0:T(8,128)(2,1)}, u32[]{:S(2)}) copy-start(bf16[1,2048,768]{2,1,0:T(8,128)(2,1)} %param.10) | copy-start | bytes 9437188
  76.9 1.9 %copy-start.2 = (bf16[1,768,2048]{2,1,0:T(8,128)(2,1)S(1)}, bf16[1,768,2048]{2,1,0:T(8,128)(2,1)}, u32[]{:S(2)}) copy-start(bf16[1,768,2048]{2,1,0:T(8,128)(2,1)} %param.12) | copy-start | bytes 9437188

commit v3 on v2

--- a/solution.py
+++ b/solution.py
@@ -7,6 +7,7 @@
 
 DEPTH = 8
 PLANE = 16
+EXPERTS = 128
 CAPACITY = 2
 PLANE_STEP = 15
 DEPTH_STEP = 3
@@ -53,7 +54,12 @@
     notes = notes.astype(F32)
     lane = iota((LINE, SLOTS), 1)
     row = iota((LINE, SLOTS), 0)
-    named = ((lane // EACH * PLANE_STEP % PLANE) * DEPTH + depth).astype(F32)
+    member_of = lane // EACH
+    core, place = depth // EXPERTS, depth % EXPERTS
+    here = (member_of * PLANE_STEP % PLANE) * DEPTH + place % DEPTH
+    other = (place // (4 * DEPTH)) * (4 * DEPTH) + (place // DEPTH % 2) * DEPTH
+    other = other + (member_of % 2) * (2 * DEPTH) + member_of // 2
+    named = jnp.where(core == 0, here, other).astype(F32)
     matches = []
     weight = jnp.zeros((LINE, SLOTS), F32)
     member = jnp.zeros((LINE, SLOTS), F32)
@@ -167,15 +173,34 @@
 def local(tokens, expert_ids, gate_values, w_gate, w_up, w_down, cotangent):
     total = 2 * WIDTH + NOTES
     place = lax.axis_index("expert")
-    depth = (place % DEPTH).astype(jnp.int32).reshape(1)
+    depth = (lax.axis_index("dp") * EXPERTS + place).astype(jnp.int32).reshape(1)
     spots = [PLANE_STEP * spot % PLANE for spot in range(PLANE)]
     levels = [DEPTH_STEP * level % DEPTH for level in range(DEPTH)]
     planes = [[spot * DEPTH + level for spot in spots] for level in range(DEPTH)]
     lines = [[spot * DEPTH + level for level in levels] for spot in range(PLANE)]
 
+    def at(row, column_high, column_low, level):
+        return EXPERTS + (row * 4 + column_high * 2 + column_low) * DEPTH + level
+
+    planes += [
+        [at(row, high, low, level) for level in range(DEPTH) for high in range(2)]
+        for row in range(4)
+        for low in range(2)
+    ]
+    lines += [
+        [at(row, high, low, level) for row in range(4) for low in range(2)]
+        for high in range(2)
+        for level in range(DEPTH)
+    ]
+
     def exchange(blocks, groups):
         return lax.all_to_all(
-            blocks, "expert", split_axis=0, concat_axis=0, tiled=True, axis_index_groups=groups
+            blocks,
+            ("dp", "expert"),
+            split_axis=0,
+            concat_axis=0,
+            tiled=True,
+            axis_index_groups=groups,
         )
 
     def near(array):

time: 148 us -> 129 us (0.87)
  waiting for transfers between devices: 28 us -> 17.9 us
  blocking collectives: 93.1 us -> 84.1 us
    all_to_all x1, waiting for transfers between devices: 28 us -> 17.9 us  [exchange(): lax.all_to_all(blocks, ('dp', 'expert'), split_axis=0, concat_axis=0, til...]
    all_to_all x3, blocking collectives: 93.1 us -> 84.1 us  [exchange(): lax.all_to_all(blocks, ('dp', 'expert'), split_axis=0, concat_axis=0, til...]
where the time goes in v3:
time: 129 us; the launch traced here: 128 us
  blocking collectives  84.1 us (65%)
  waiting for transfers between devices  17.9 us (14%)
  Pallas kernels  12.2 us (9%)
  starting transfers between devices  8.57 us (7%)
  local copies, waits for them, and re-layouts  4.94 us (4%)
    all_to_all x3, blocking collectives, exchange(): lax.all_to_all(blocks, ('dp', 'expert'), split_axis=0, concat_axis=0, til...  84.1 us
    all_to_all x1, waiting for transfers between devices, exchange(): lax.all_to_all(blocks, ('dp', 'expert'), split_axis=0, concat_axis=0, til...  17.9 us
    all_to_all x1, starting transfers between devices, exchange(): lax.all_to_all(blocks, ('dp', 'expert'), split_axis=0, concat_axis=0, til...  8.57 us
    pallas_call x1, Pallas kernels, local(): pl.pallas_call(expert_kernel, out_shape=pltpu.VMEM((SLOTS, 2 * WIDTH), BF...  7.5 us
    unnamed x14, local copies, waits for them, and re-layouts  4.94 us
  transfers between devices with their start and end apart: 1, of which 1 were waited for; matrix products, arithmetic and copies ran while one was open for 0% of the time, Pallas kernels for 0%

profile of v3, /device:TPU:32, one launch (start us, length us, event | category | flops | bytes accessed | tf_op | source)
XLA Modules:
  0.0 128.3 jit_solution(9901269774420113304)
XLA Ops:
  0.6 0.0 copy-start.3
  0.6 0.8 copy-done.3
  1.5 0.0 copy-start.4
  1.5 0.8 copy-done.4
  2.3 0.0 copy-start.5
  2.3 0.7 copy-done.5
  3.0 0.0 copy-start.6
  3.0 0.7 copy-done.6
  3.7 1.1 pack.1
  4.7 8.6 %all-to-all-start = ((bf16[8,16,4224]{2,1,0:T(8,128)(2,1)}), bf16[8,16,4224]{2,1,0:T(8,128)(2,1)S(1)}, u32[]{:S(2)}, u32[]{:S(2)}) async-start(bf16[8,16,4224]{2,1,0:T(8,128)(2,1)} %bitcast.3), calls=%async_computation | async-start | bytes 2162688 | tf_op jit(solution)/shard_map/all_to_all | solution.py:197
  13.3 17.9 %all-to-all-done = bf16[8,16,4224]{2,1,0:T(8,128)(2,1)S(1)} async-done(((bf16[8,16,4224]{2,1,0:T(8,128)(2,1)}), bf16[8,16,4224]{2,1,0:T(8,128)(2,1)S(1)}, u32[]{:S(2)}, u32[]{:S(2)}) %all-to-all-start) | async-done | bytes 1081376 | tf_op jit(solution)/shard_map/all_to_all | solution.py:197
  31.2 0.0 copy-start.1
  31.2 1.1 dispatch.1
  32.3 0.0 copy-start
  32.3 31.8 %all_to_all.20 = bf16[16,16,4096]{2,1,0:T(8,128)(2,1)S(1)} all-to-all(bf16[16,16,4096]{2,1,0:T(8,128)(2,1)S(1)} %bitcast.17), channel_id=1, replica_groups={{0,240,224,208,192,176,160,144,128,112,96,80,64,48,32,16},{2,242,226,21..., dimensions={0} | all-to-all | bytes 4194304 | tf_op jit(solution)/shard_map/all_to_all | solution.py:197
  64.1 0.0 copy-done.1
  64.1 0.0 copy-done
  64.1 0.0 copy-start.2
  64.1 1.9 %copy-done.2 = bf16[1,768,2048]{2,1,0:T(8,128)(2,1)S(1)} copy-done((bf16[1,768,2048]{2,1,0:T(8,128)(2,1)S(1)}, bf16[1,768,2048]{2,1,0:T(8,128)(2,1)}, u32[]{:S(2)}) %copy-start.2) | copy-done | bytes 3145752
  66.0 7.5 %expert.1 = bf16[256,4096]{1,0:T(8,128)(2,1)S(1)} custom-call(bf16[256,4096]{1,0:T(8,128)(2,1)S(1)} %bitcast.18, bf16[2048,768]{1,0:T(8,128)(2,1)S(1)} %bitcast.21, bf16[2048,768]{1,0:T(8,128)(2,1)S(1)} %bitcast.22, bf16[768,2048]{1,0:T(8,128)(2,1)S(1)} %bitcast.23), custom_call_target="tpu_custom_call" | custom-call | tf_op jit(solution)/shard_map/expert/pallas_call | solution.py:231
  73.5 29.9 %all_to_all.21 = bf16[16,16,4096]{2,1,0:T(8,128)(2,1)S(1)} all-to-all(bf16[16,16,4096]{2,1,0:T(8,128)(2,1)S(1)} %bitcast.19), channel_id=1, replica_groups={{0,240,224,208,192,176,160,144,128,112,96,80,64,48,32,16},{2,242,226,21..., dimensions={0} | all-to-all | bytes 4194304 | tf_op jit(solution)/shard_map/all_to_all | solution.py:197
  103.4 1.7 %combine.1 = bf16[128,4224]{1,0:T(8,128)(2,1)S(1)} custom-call(s32[1]{0:T(128)} %bitcast.depth_ref, bf16[128,4224]{1,0:T(8,128)(2,1)S(1)} %bitcast.15, bf16[256,4096]{1,0:T(8,128)(2,1)S(1)} %bitcast.16), custom_call_target="tpu_custom_call" | custom-call | tf_op jit(solution)/shard_map/combine/pallas_call | solution.py:247
  105.1 22.3 %all_to_all.22.parts_ref = bf16[8,16,4224]{2,1,0:T(8,128)(2,1)S(1)} all-to-all(bf16[8,16,4224]{2,1,0:T(8,128)(2,1)S(1)} %bitcast.20), channel_id=1, replica_groups={{0,6,12,2,8,14,4,10},{16,22,28,18,24,30,20,26},{32,38,44,34,40,46,36,42..., dimensions={0} | all-to-all | bytes 2162688 | tf_op jit(solution)/shard_map/all_to_all | solution.py:197
  127.5 0.8 finish.1
Async XLA Ops:
  0.6 0.8 copy-start.3
  1.5 0.8 copy-start.4
  2.3 0.7 copy-start.5
  3.0 0.7 copy-start.6
  4.7 26.4 %all-to-all-start = ((bf16[8,16,4224]{2,1,0:T(8,128)(2,1)}), bf16[8,16,4224]{2,1,0:T(8,128)(2,1)S(1)}, u32[]{:S(2)}, u32[]{:S(2)}) async-start(bf16[8,16,4224]{2,1,0:T(8,128)(2,1)} %bitcast.3), calls=%async_computation | async-start | bytes 2162688 | tf_op jit(solution)/shard_map/all_to_all | solution.py:197
  31.2 33.0 %copy-start.1 = (bf16[1,2048,768]{2,1,0:T(8,128)(2,1)S(1)}, bf16[1,2048,768]{2,1,0:T(8,128)(2,1)}, u32[]{:S(2)}) copy-start(bf16[1,2048,768]{2,1,0:T(8,128)(2,1)} %param.11) | copy-start | bytes 9437188
  32.3 31.8 %copy-start = (bf16[1,2048,768]{2,1,0:T(8,128)(2,1)S(1)}, bf16[1,2048,768]{2,1,0:T(8,128)(2,1)}, u32[]{:S(2)}) copy-start(bf16[1,2048,768]{2,1,0:T(8,128)(2,1)} %param.10) | copy-start | bytes 9437188
  64.1 1.9 %copy-start.2 = (bf16[1,768,2048]{2,1,0:T(8,128)(2,1)S(1)}, bf16[1,768,2048]{2,1,0:T(8,128)(2,1)}, u32[]{:S(2)}) copy-start(bf16[1,768,2048]{2,1,0:T(8,128)(2,1)} %param.12) | copy-start | bytes 9437188

commit v4 on v3

--- a/solution.py
+++ b/solution.py
@@ -37,17 +37,33 @@
     return high, middle, low
 
 
-def pack_kernel(tokens_ref, cotangent_ref, ids_ref, gates_ref, out_ref):
-    high, middle, low = parts_of(gates_ref[...])
+def pack_kernel(
+    tokens_hbm, cotangent_hbm, ids_hbm, gates_hbm, out_ref, tokens, cotangent, ids, gates, sems
+):
+    copies = [
+        pltpu.make_async_copy(ids_hbm, ids, sems.at[0]),
+        pltpu.make_async_copy(gates_hbm, gates, sems.at[1]),
+        pltpu.make_async_copy(tokens_hbm, tokens, sems.at[2]),
+        pltpu.make_async_copy(cotangent_hbm, cotangent, sems.at[3]),
+    ]
+    for copy in copies:
+        copy.start()
+    copies[0].wait()
+    copies[1].wait()
+    high, middle, low = parts_of(gates[...])
     columns = jnp.concatenate(
-        [ids_ref[...].astype(F32), high.astype(F32), middle.astype(F32), low.astype(F32)], axis=0
+        [ids[...].astype(F32), high.astype(F32), middle.astype(F32), low.astype(F32)], axis=0
     )
     columns = jnp.concatenate([columns, jnp.zeros((NOTES - 4 * TOP, ROWS), F32)], axis=0)
     notes = columns.T.astype(BF)
     for start in range(0, LINE, ROWS):
-        out_ref[start : start + ROWS, :WIDTH] = tokens_ref[...]
-        out_ref[start : start + ROWS, WIDTH : 2 * WIDTH] = cotangent_ref[...]
         out_ref[start : start + ROWS, 2 * WIDTH :] = notes
+    copies[2].wait()
+    for start in range(0, LINE, ROWS):
+        out_ref[start : start + ROWS, :WIDTH] = tokens[...]
+    copies[3].wait()
+    for start in range(0, LINE, ROWS):
+        out_ref[start : start + ROWS, WIDTH : 2 * WIDTH] = cotangent[...]
 
 
 def tables(depth, notes):
@@ -57,8 +73,8 @@
     member_of = lane // EACH
     core, place = depth // EXPERTS, depth % EXPERTS
     here = (member_of * PLANE_STEP % PLANE) * DEPTH + place % DEPTH
-    other = (place // (4 * DEPTH)) * (4 * DEPTH) + (place // DEPTH % 2) * DEPTH
-    other = other + (member_of % 2) * (2 * DEPTH) + member_of // 2
+    other = (place // (2 * DEPTH)) * (2 * DEPTH)
+    other = other + (member_of % 2) * DEPTH + member_of // 2
     named = jnp.where(core == 0, here, other).astype(F32)
     matches = []
     weight = jnp.zeros((LINE, SLOTS), F32)
@@ -105,22 +121,15 @@
     return lax.dot_general(left, right, (((1,), (1,)), ((), ())), preferred_element_type=F32)
 
 
-def expert_kernel(rows, gate_hbm, up_hbm, down_hbm, out, gate, up, down, sems):
-    copies = [
-        pltpu.make_async_copy(gate_hbm, gate, sems.at[0]),
-        pltpu.make_async_copy(up_hbm, up, sems.at[1]),
-        pltpu.make_async_copy(down_hbm, down, sems.at[2]),
-    ]
-    for copy in copies:
-        copy.start()
+def expert_kernel(rows, gate, up, down_hbm, out, down, sem):
+    copy = pltpu.make_async_copy(down_hbm, down, sem)
+    copy.start()
     inputs = rows[:, :WIDTH]
-    copies[0].wait()
     pre_gate = jnp.dot(inputs, gate[...], preferred_element_type=F32)
-    copies[1].wait()
     pre_up = jnp.dot(inputs, up[...], preferred_element_type=F32)
     sigmoid = jax.nn.sigmoid(pre_gate)
     hidden = (pre_gate * sigmoid * pre_up).astype(BF)
-    copies[2].wait()
+    copy.wait()
     out[:, :WIDTH] = jnp.dot(hidden, down[...], preferred_element_type=F32).astype(BF)
     grad_hidden = dot_t(rows[:, WIDTH:], down[...])
     grad_gate = (grad_hidden * pre_up * sigmoid * (1.0 + pre_gate * (1.0 - sigmoid))).astype(BF)
@@ -183,13 +192,13 @@
         return EXPERTS + (row * 4 + column_high * 2 + column_low) * DEPTH + level
 
     planes += [
-        [at(row, high, low, level) for level in range(DEPTH) for high in range(2)]
+        [at(row, high, low, level) for level in range(DEPTH) for low in range(2)]
         for row in range(4)
-        for low in range(2)
+        for high in range(2)
     ]
     lines += [
-        [at(row, high, low, level) for row in range(4) for low in range(2)]
-        for high in range(2)
+        [at(row, high, low, level) for row in range(4) for high in range(2)]
+        for low in range(2)
         for level in range(DEPTH)
     ]
 
@@ -206,17 +215,27 @@
     def near(array):
         return pltpu.with_memory_space_constraint(array, pltpu.VMEM)
 
+    def far(array):
+        return pltpu.with_memory_space_constraint(array, pltpu.HBM)
+
     vmem = pl.BlockSpec(memory_space=pltpu.VMEM)
     smem = pl.BlockSpec(memory_space=pltpu.SMEM)
     anywhere = pl.BlockSpec(memory_space=pl.ANY)
     packed = pl.pallas_call(
         pack_kernel,
         out_shape=pltpu.VMEM((LINE, total), BF),
-        in_specs=[vmem] * 4,
+        in_specs=[anywhere] * 4,
         out_specs=vmem,
+        scratch_shapes=[
+            pltpu.VMEM((ROWS, WIDTH), BF),
+            pltpu.VMEM((ROWS, WIDTH), BF),
+            pltpu.VMEM((TOP, ROWS), jnp.int32),
+            pltpu.VMEM((TOP, ROWS), F32),
+            pltpu.SemaphoreType.DMA((4,)),
+        ],
         name="pack",
         compiler_params=pltpu.CompilerParams(vmem_limit_bytes=8 * MIB),
-    )(tokens, cotangent, expert_ids.T, gate_values.T)
+    )(far(tokens), far(cotangent), far(expert_ids.T), far(gate_values.T))
     line = near(exchange(packed.reshape(DEPTH, ROWS, total), lines).reshape(LINE, total))
     sent = pl.pallas_call(
         dispatch_kernel,
@@ -231,17 +250,15 @@
     output = pl.pallas_call(
         expert_kernel,
         out_shape=pltpu.VMEM((SLOTS, 2 * WIDTH), BF),
-        in_specs=[vmem, anywhere, anywhere, anywhere],
+        in_specs=[vmem, vmem, vmem, anywhere],
         out_specs=vmem,
         scratch_shapes=[
-            pltpu.VMEM((WIDTH, HIDDEN), BF),
-            pltpu.VMEM((WIDTH, HIDDEN), BF),
             pltpu.VMEM((HIDDEN, WIDTH), BF),
-            pltpu.SemaphoreType.DMA((3,)),
+            pltpu.SemaphoreType.DMA,
         ],
         name="expert",
         compiler_params=pltpu.CompilerParams(vmem_limit_bytes=28 * MIB),
-    )(received, w_gate[0], w_up[0], w_down[0])
+    )(received, near(w_gate[0]), near(w_up[0]), far(w_down[0]))
     back = exchange(output.reshape(PLANE, EACH, 2 * WIDTH), planes)
     back = near(back.reshape(SLOTS, 2 * WIDTH))
     parts = pl.pallas_call(

time: 129 us -> 123 us (0.953)
  local copies, waits for them, and re-layouts: 4.94 us -> 0.01 us
    unnamed x14 -> x4, local copies, waits for them, and re-layouts: 4.94 us -> 0.01 us
    pallas_call x1, Pallas kernels: 7.5 us -> 6.11 us  [local(): pl.pallas_call(expert_kernel, out_shape=pltpu.VMEM((SLOTS, 2 * WIDTH), BF...]
where the time goes in v4:
time: 123 us; the launch traced here: 122 us
  blocking collectives  83.3 us (68%)
  waiting for transfers between devices  17.9 us (15%)
  Pallas kernels  11.7 us (10%)
  starting transfers between devices  8.58 us (7%)
    all_to_all x3, blocking collectives, exchange(): lax.all_to_all(blocks, ('dp', 'expert'), split_axis=0, concat_axis=0, til...  83.3 us
    all_to_all x1, waiting for transfers between devices, exchange(): lax.all_to_all(blocks, ('dp', 'expert'), split_axis=0, concat_axis=0, til...  17.9 us
    all_to_all x1, starting transfers between devices, exchange(): lax.all_to_all(blocks, ('dp', 'expert'), split_axis=0, concat_axis=0, til...  8.58 us
    pallas_call x1, Pallas kernels, local(): pl.pallas_call(expert_kernel, out_shape=pltpu.VMEM((SLOTS, 2 * WIDTH), BF...  6.11 us
  transfers between devices with their start and end apart: 1, of which 1 were waited for; matrix products, arithmetic and copies ran while one was open for 0% of the time, Pallas kernels for 0%

profile of v4, /device:TPU:32, one launch (start us, length us, event | category | flops | bytes accessed | tf_op | source)
XLA Modules:
  0.0 122.1 jit_solution(4851099135028474244)
XLA Ops:
  0.6 2.0 %pack.1 = bf16[128,4224]{1,0:T(8,128)(2,1)} custom-call(bf16[16,2048]{1,0:T(8,128)(2,1)} %tokens_hbm.1, bf16[16,2048]{1,0:T(8,128)(2,1)} %cotangent_hbm.1, s32[8,16]{1,0:T(8,128)} %bitcast.24, f32[8,16]{1,0:T(8,128)} %bitcast.25), custom_call_target="tpu_custom_call" | custom-call | tf_op jit(solution)/shard_map/pack/pallas_call | solution.py:224
  2.6 8.6 %all-to-all-start = ((bf16[8,16,4224]{2,1,0:T(8,128)(2,1)}), bf16[8,16,4224]{2,1,0:T(8,128)(2,1)S(1)}, u32[]{:S(2)}, u32[]{:S(2)}) async-start(bf16[8,16,4224]{2,1,0:T(8,128)(2,1)} %bitcast.3), calls=%async_computation | async-start | bytes 2162688 | tf_op jit(solution)/shard_map/all_to_all | solution.py:206
  11.2 17.9 %all-to-all-done = bf16[8,16,4224]{2,1,0:T(8,128)(2,1)S(1)} async-done(((bf16[8,16,4224]{2,1,0:T(8,128)(2,1)}), bf16[8,16,4224]{2,1,0:T(8,128)(2,1)S(1)}, u32[]{:S(2)}, u32[]{:S(2)}) %all-to-all-start) | async-done | bytes 1081376 | tf_op jit(solution)/shard_map/all_to_all | solution.py:206
  29.0 0.0 copy-start.1
  29.0 1.1 dispatch.1
  30.2 0.0 copy-start
  30.2 30.9 %all_to_all.20 = bf16[16,16,4096]{2,1,0:T(8,128)(2,1)S(1)} all-to-all(bf16[16,16,4096]{2,1,0:T(8,128)(2,1)S(1)} %bitcast.17), channel_id=1, replica_groups={{0,240,224,208,192,176,160,144,128,112,96,80,64,48,32,16},{2,242,226,21..., dimensions={0} | all-to-all | bytes 4194304 | tf_op jit(solution)/shard_map/all_to_all | solution.py:206
  61.1 0.0 copy-done.1
  61.1 0.0 copy-done
  61.1 6.1 %expert.1 = bf16[256,4096]{1,0:T(8,128)(2,1)S(1)} custom-call(bf16[256,4096]{1,0:T(8,128)(2,1)S(1)} %bitcast.18, bf16[2048,768]{1,0:T(8,128)(2,1)S(1)} %bitcast.21, bf16[2048,768]{1,0:T(8,128)(2,1)S(1)} %bitcast.22, bf16[768,2048]{1,0:T(8,128)(2,1)} %bitcast.23), custom_call_target="tpu_custom_call" | custom-call | tf_op jit(solution)/shard_map/expert/pallas_call | solution.py:250
  67.2 29.8 %all_to_all.21 = bf16[16,16,4096]{2,1,0:T(8,128)(2,1)S(1)} all-to-all(bf16[16,16,4096]{2,1,0:T(8,128)(2,1)S(1)} %bitcast.19), channel_id=1, replica_groups={{0,240,224,208,192,176,160,144,128,112,96,80,64,48,32,16},{2,242,226,21..., dimensions={0} | all-to-all | bytes 4194304 | tf_op jit(solution)/shard_map/all_to_all | solution.py:206
  97.0 1.7 %combine.1 = bf16[128,4224]{1,0:T(8,128)(2,1)S(1)} custom-call(s32[1]{0:T(128)} %bitcast.depth_ref, bf16[128,4224]{1,0:T(8,128)(2,1)S(1)} %bitcast.15, bf16[256,4096]{1,0:T(8,128)(2,1)S(1)} %bitcast.16), custom_call_target="tpu_custom_call" | custom-call | tf_op jit(solution)/shard_map/combine/pallas_call | solution.py:264
  98.7 22.6 %all_to_all.22.parts_ref = bf16[8,16,4224]{2,1,0:T(8,128)(2,1)S(1)} all-to-all(bf16[8,16,4224]{2,1,0:T(8,128)(2,1)S(1)} %bitcast.20), channel_id=1, replica_groups={{0,6,12,2,8,14,4,10},{16,22,28,18,24,30,20,26},{32,38,44,34,40,46,36,42..., dimensions={0} | all-to-all | bytes 2162688 | tf_op jit(solution)/shard_map/all_to_all | solution.py:206
  121.3 0.8 finish.1
Async XLA Ops:
  2.6 26.4 %all-to-all-start = ((bf16[8,16,4224]{2,1,0:T(8,128)(2,1)}), bf16[8,16,4224]{2,1,0:T(8,128)(2,1)S(1)}, u32[]{:S(2)}, u32[]{:S(2)}) async-start(bf16[8,16,4224]{2,1,0:T(8,128)(2,1)} %bitcast.3), calls=%async_computation | async-start | bytes 2162688 | tf_op jit(solution)/shard_map/all_to_all | solution.py:206
  29.0 32.0 %copy-start.1 = (bf16[1,2048,768]{2,1,0:T(8,128)(2,1)S(1)}, bf16[1,2048,768]{2,1,0:T(8,128)(2,1)}, u32[]{:S(2)}) copy-start(bf16[1,2048,768]{2,1,0:T(8,128)(2,1)} %param.11) | copy-start | bytes 9437188
  30.2 30.9 %copy-start = (bf16[1,2048,768]{2,1,0:T(8,128)(2,1)S(1)}, bf16[1,2048,768]{2,1,0:T(8,128)(2,1)}, u32[]{:S(2)}) copy-start(bf16[1,2048,768]{2,1,0:T(8,128)(2,1)} %param.10) | copy-start | bytes 9437188

commit v5 on v4

--- a/solution.py
+++ b/solution.py
@@ -9,7 +9,7 @@
 PLANE = 16
 EXPERTS = 128
 CAPACITY = 2
-PLANE_STEP = 15
+PLANE_STEP = 7
 DEPTH_STEP = 3
 ROWS = 16
 TOP = 8
@@ -22,6 +22,7 @@
 BF = jnp.bfloat16
 F32 = jnp.float32
 COLUMNS = 512
+STAGGER = 17500
 MIB = 1024 * 1024
 
 
@@ -38,7 +39,7 @@
 
 
 def pack_kernel(
-    tokens_hbm, cotangent_hbm, ids_hbm, gates_hbm, out_ref, tokens, cotangent, ids, gates, sems
+    depth_ref, tokens_hbm, cotangent_hbm, ids_hbm, gates_hbm, out_ref, tokens, cotangent, ids, gates, sems
 ):
     copies = [
         pltpu.make_async_copy(ids_hbm, ids, sems.at[0]),
@@ -48,6 +49,11 @@
     ]
     for copy in copies:
         copy.start()
+
+    @pl.when(depth_ref[0] >= EXPERTS)
+    def _():
+        pl.delay(STAGGER)
+
     copies[0].wait()
     copies[1].wait()
     high, middle, low = parts_of(gates[...])
@@ -71,11 +77,8 @@
     lane = iota((LINE, SLOTS), 1)
     row = iota((LINE, SLOTS), 0)
     member_of = lane // EACH
-    core, place = depth // EXPERTS, depth % EXPERTS
-    here = (member_of * PLANE_STEP % PLANE) * DEPTH + place % DEPTH
-    other = (place // (2 * DEPTH)) * (2 * DEPTH)
-    other = other + (member_of % 2) * DEPTH + member_of // 2
-    named = jnp.where(core == 0, here, other).astype(F32)
+    place = depth % EXPERTS
+    named = ((member_of * PLANE_STEP % PLANE) * DEPTH + place % DEPTH).astype(F32)
     matches = []
     weight = jnp.zeros((LINE, SLOTS), F32)
     member = jnp.zeros((LINE, SLOTS), F32)
@@ -188,19 +191,8 @@
     planes = [[spot * DEPTH + level for spot in spots] for level in range(DEPTH)]
     lines = [[spot * DEPTH + level for level in levels] for spot in range(PLANE)]
 
-    def at(row, column_high, column_low, level):
-        return EXPERTS + (row * 4 + column_high * 2 + column_low) * DEPTH + level
-
-    planes += [
-        [at(row, high, low, level) for level in range(DEPTH) for low in range(2)]
-        for row in range(4)
-        for high in range(2)
-    ]
-    lines += [
-        [at(row, high, low, level) for row in range(4) for high in range(2)]
-        for low in range(2)
-        for level in range(DEPTH)
-    ]
+    planes += [[EXPERTS + member for member in group] for group in planes]
+    lines += [[EXPERTS + member for member in group] for group in lines]
 
     def exchange(blocks, groups):
         return lax.all_to_all(
@@ -224,7 +216,7 @@
     packed = pl.pallas_call(
         pack_kernel,
         out_shape=pltpu.VMEM((LINE, total), BF),
-        in_specs=[anywhere] * 4,
+        in_specs=[smem] + [anywhere] * 4,
         out_specs=vmem,
         scratch_shapes=[
             pltpu.VMEM((ROWS, WIDTH), BF),
@@ -235,7 +227,7 @@
         ],
         name="pack",
         compiler_params=pltpu.CompilerParams(vmem_limit_bytes=8 * MIB),
-    )(far(tokens), far(cotangent), far(expert_ids.T), far(gate_values.T))
+    )(depth, far(tokens), far(cotangent), far(expert_ids.T), far(gate_values.T))
     line = near(exchange(packed.reshape(DEPTH, ROWS, total), lines).reshape(LINE, total))
     sent = pl.pallas_call(
         dispatch_kernel,

time: 123 us -> 120 us (0.976)
  the two profiles are of different devices: /device:TPU:32 before, /device:TPU:1 now
where the time goes in v5:
time: 120 us; the launch traced here: 119 us
  blocking collectives  91.2 us (76%)
  Pallas kernels  27.4 us (23%)
    all_to_all x4, blocking collectives, exchange(): lax.all_to_all(blocks, ('dp', 'expert'), split_axis=0, concat_axis=0, til...  91.2 us
    pallas_call x1, Pallas kernels, local(): pl.pallas_call(pack_kernel, out_shape=pltpu.VMEM((LINE, total), BF), in_s...  17.7 us
    pallas_call x1, Pallas kernels, local(): pl.pallas_call(expert_kernel, out_shape=pltpu.VMEM((SLOTS, 2 * WIDTH), BF...  6.11 us

profile of v5, /device:TPU:1, one launch (start us, length us, event | category | flops | bytes accessed | tf_op | source)
XLA Modules:
  0.0 119.3 jit_solution(11043827604795069740)
XLA Ops:
  0.6 17.7 %pack.1 = bf16[128,4224]{1,0:T(8,128)(2,1)S(1)} custom-call(s32[1]{0:T(128)} %bitcast.depth_ref, bf16[16,2048]{1,0:T(8,128)(2,1)} %tokens_hbm.1, bf16[16,2048]{1,0:T(8,128)(2,1)} %cotangent_hbm.1, s32[8,16]{1,0:T(8,128)} %bitcast.25, f32[8,16]{1,0:T(8,128)} %bitcast.26), custom_call_target="tpu_custom_call" | custom-call | tf_op jit(solution)/shard_map/pack/pallas_call | solution.py:216
  18.3 26.8 %all_to_all.20 = bf16[8,16,4224]{2,1,0:T(8,128)(2,1)S(1)} all-to-all(bf16[8,16,4224]{2,1,0:T(8,128)(2,1)S(1)} %bitcast.20), channel_id=1, replica_groups={{0,6,12,2,8,14,4,10},{16,22,28,18,24,30,20,26},{32,38,44,34,40,46,36,42..., dimensions={0} | all-to-all | bytes 2162688 | tf_op jit(solution)/shard_map/all_to_all | solution.py:198
  45.2 0.0 copy-start.1
  45.2 1.1 dispatch.1
  46.3 0.0 copy-start
  46.3 23.1 %all_to_all.21 = bf16[16,16,4096]{2,1,0:T(8,128)(2,1)S(1)} all-to-all(bf16[16,16,4096]{2,1,0:T(8,128)(2,1)S(1)} %bitcast.17), channel_id=1, replica_groups={{0,112,224,80,192,48,160,16,128,240,96,208,64,176,32,144},{2,114,226,82..., dimensions={0} | all-to-all | bytes 4194304 | tf_op jit(solution)/shard_map/all_to_all | solution.py:198
  69.5 0.0 copy-done.1
  69.5 0.0 copy-done
  69.5 6.1 %expert.1 = bf16[256,4096]{1,0:T(8,128)(2,1)S(1)} custom-call(bf16[256,4096]{1,0:T(8,128)(2,1)S(1)} %bitcast.18, bf16[2048,768]{1,0:T(8,128)(2,1)S(1)} %bitcast.22, bf16[2048,768]{1,0:T(8,128)(2,1)S(1)} %bitcast.23, bf16[768,2048]{1,0:T(8,128)(2,1)} %bitcast.24), custom_call_target="tpu_custom_call" | custom-call | tf_op jit(solution)/shard_map/expert/pallas_call | solution.py:242
  75.6 20.5 %all_to_all.22 = bf16[16,16,4096]{2,1,0:T(8,128)(2,1)S(1)} all-to-all(bf16[16,16,4096]{2,1,0:T(8,128)(2,1)S(1)} %bitcast.19), channel_id=1, replica_groups={{0,112,224,80,192,48,160,16,128,240,96,208,64,176,32,144},{2,114,226,82..., dimensions={0} | all-to-all | bytes 4194304 | tf_op jit(solution)/shard_map/all_to_all | solution.py:198
  96.1 1.7 %combine.1 = bf16[128,4224]{1,0:T(8,128)(2,1)S(1)} custom-call(s32[1]{0:T(128)} %bitcast.depth_ref, bf16[128,4224]{1,0:T(8,128)(2,1)S(1)} %bitcast.15, bf16[256,4096]{1,0:T(8,128)(2,1)S(1)} %bitcast.16), custom_call_target="tpu_custom_call" | custom-call | tf_op jit(solution)/shard_map/combine/pallas_call | solution.py:256
  97.8 20.7 %all_to_all.23.parts_ref = bf16[8,16,4224]{2,1,0:T(8,128)(2,1)S(1)} all-to-all(bf16[8,16,4224]{2,1,0:T(8,128)(2,1)S(1)} %bitcast.21), channel_id=1, replica_groups={{0,6,12,2,8,14,4,10},{16,22,28,18,24,30,20,26},{32,38,44,34,40,46,36,42..., dimensions={0} | all-to-all | bytes 2162688 | tf_op jit(solution)/shard_map/all_to_all | solution.py:198
  118.5 0.8 finish.1
Async XLA Ops:
  45.2 24.3 %copy-start.1 = (bf16[1,2048,768]{2,1,0:T(8,128)(2,1)S(1)}, bf16[1,2048,768]{2,1,0:T(8,128)(2,1)}, u32[]{:S(2)}) copy-start(bf16[1,2048,768]{2,1,0:T(8,128)(2,1)} %param.11) | copy-start | bytes 9437188
  46.3 23.2 %copy-start = (bf16[1,2048,768]{2,1,0:T(8,128)(2,1)S(1)}, bf16[1,2048,768]{2,1,0:T(8,128)(2,1)}, u32[]{:S(2)}) copy-start(bf16[1,2048,768]{2,1,0:T(8,128)(2,1)} %param.10) | copy-start | bytes 9437188

commit v6 on v5

--- a/solution.py
+++ b/solution.py
@@ -79,9 +79,8 @@
     member_of = lane // EACH
     place = depth % EXPERTS
     named = ((member_of * PLANE_STEP % PLANE) * DEPTH + place % DEPTH).astype(F32)
-    matches = []
     weight = jnp.zeros((LINE, SLOTS), F32)
-    member = jnp.zeros((LINE, SLOTS), F32)
+    pick = jnp.full((LINE, SLOTS), -1.0, F32)
     for k in range(TOP):
         match = notes[:, k : k + 1] == named
         gate = (
@@ -90,8 +89,8 @@
             + notes[:, 3 * TOP + k : 3 * TOP + k + 1]
         )
         weight = jnp.where(match, gate, weight)
-        member = jnp.where(match, 1.0, member)
-        matches.append(match)
+        pick = jnp.where(match, float(k), pick)
+    member = jnp.where(pick >= 0.0, 1.0, 0.0)
     left = iota((LINE, LINE), 0)
     right = iota((LINE, LINE), 1)
     ahead = ((left // ROWS == right // ROWS) & (right < left)).astype(F32).astype(BF)
@@ -100,12 +99,14 @@
         ranked == (lane % CAPACITY).astype(F32)
     )
     hit = jnp.where(here, member, 0.0)
-    return hit, hit * weight, matches
-
-
-def dispatch_kernel(depth_ref, line_ref, out_ref):
+    return hit, hit * weight, jnp.where(hit > 0.0, pick, -1.0)
+
+
+def dispatch_kernel(depth_ref, line_ref, out_ref, weight_ref, pick_ref):
     notes = line_ref[:, 2 * WIDTH :]
-    hit, weight, _ = tables(depth_ref[0], notes)
+    hit, weight, pick = tables(depth_ref[0], notes)
+    weight_ref[...] = weight
+    pick_ref[...] = pick
     select = hit.T.astype(BF)
     gates = jnp.sum(weight.T, axis=1, keepdims=True)
     for start in range(0, WIDTH, COLUMNS):
@@ -140,10 +141,10 @@
     out[:, WIDTH:] = (dot_t(grad_gate, gate[...]) + dot_t(grad_up, up[...])).astype(BF)
 
 
-def combine_kernel(depth_ref, line_ref, back_ref, out_ref):
-    hit, weight, matches = tables(depth_ref[0], line_ref[:, 2 * WIDTH :])
-    select = hit.astype(BF)
-    high, middle, low = parts_of(weight)
+def combine_kernel(weight_ref, pick_ref, line_ref, back_ref, out_ref):
+    pick = pick_ref[...]
+    select = jnp.where(pick >= 0.0, 1.0, 0.0).astype(BF)
+    high, middle, low = parts_of(weight_ref[...])
     scores = jnp.zeros((LINE, SLOTS), F32)
     for start in range(0, WIDTH, COLUMNS):
         block = back_ref[:, start : start + COLUMNS]
@@ -159,11 +160,10 @@
         out_ref[:, start : start + COLUMNS] = jnp.dot(
             select, block, preferred_element_type=F32
         ).astype(BF)
-    scores = jnp.where(hit > 0.0, scores, 0.0)
     lane = iota((LINE, NOTES), 1)
     notes = jnp.zeros((LINE, NOTES), F32)
     for k in range(TOP):
-        total = jnp.sum(jnp.where(matches[k], scores, 0.0), axis=1, keepdims=True)
+        total = jnp.sum(jnp.where(pick == float(k), scores, 0.0), axis=1, keepdims=True)
         for part, value in enumerate(parts_of(total)):
             notes = jnp.where(lane == part * TOP + k, value.astype(F32), notes)
     out_ref[:, 2 * WIDTH :] = notes.astype(BF)
@@ -229,11 +229,15 @@
         compiler_params=pltpu.CompilerParams(vmem_limit_bytes=8 * MIB),
     )(depth, far(tokens), far(cotangent), far(expert_ids.T), far(gate_values.T))
     line = near(exchange(packed.reshape(DEPTH, ROWS, total), lines).reshape(LINE, total))
-    sent = pl.pallas_call(
+    sent, weight, pick = pl.pallas_call(
         dispatch_kernel,
-        out_shape=pltpu.VMEM((SLOTS, 2 * WIDTH), BF),
+        out_shape=(
+            pltpu.VMEM((SLOTS, 2 * WIDTH), BF),
+            pltpu.VMEM((LINE, SLOTS), F32),
+            pltpu.VMEM((LINE, SLOTS), F32),
+        ),
         in_specs=[smem, vmem],
-        out_specs=vmem,
+        out_specs=(vmem, vmem, vmem),
         name="dispatch",
         compiler_params=pltpu.CompilerParams(vmem_limit_bytes=16 * MIB),
     )(depth, line)
@@ -256,11 +260,11 @@
     parts = pl.pallas_call(
         combine_kernel,
         out_shape=pltpu.VMEM((LINE, total), BF),
-        in_specs=[smem, vmem, vmem],
+        in_specs=[vmem] * 4,
         out_specs=vmem,
         name="combine",
         compiler_params=pltpu.CompilerParams(vmem_limit_bytes=16 * MIB),
-    )(depth, line, back)
+    )(near(weight), near(pick), line, back)
     parts = near(exchange(parts.reshape(DEPTH, ROWS, total), lines))
     mixed_rows, row_grads, gate_grads = pl.pallas_call(
         finish_kernel,

time: 120 us -> 119 us (level)
  no operation moved by 1% of the time
where the time goes in v6:
time: 119 us
  blocking collectives  91.4 us (77%)
  Pallas kernels  27 us (23%)
    all_to_all x4, blocking collectives, exchange(): lax.all_to_all(blocks, ('dp', 'expert'), split_axis=0, concat_axis=0, til...  91.4 us
    pallas_call x1, Pallas kernels, local(): pl.pallas_call(pack_kernel, out_shape=pltpu.VMEM((LINE, total), BF), in_s...  17.7 us
    pallas_call x1, Pallas kernels, local(): pl.pallas_call(expert_kernel, out_shape=pltpu.VMEM((SLOTS, 2 * WIDTH), BF...  6.11 us

profile of v6, /device:TPU:1, one launch (start us, length us, event | category | flops | bytes accessed | tf_op | source)
XLA Modules:
  0.0 119.1 jit_solution(15393569335913439642)
XLA Ops:
  0.6 17.7 %pack.1 = bf16[128,4224]{1,0:T(8,128)(2,1)S(1)} custom-call(s32[1]{0:T(128)} %bitcast.depth_ref, bf16[16,2048]{1,0:T(8,128)(2,1)} %tokens_hbm.1, bf16[16,2048]{1,0:T(8,128)(2,1)} %cotangent_hbm.1, s32[8,16]{1,0:T(8,128)} %bitcast.25, f32[8,16]{1,0:T(8,128)} %bitcast.26), custom_call_target="tpu_custom_call" | custom-call | tf_op jit(solution)/shard_map/pack/pallas_call | solution.py:216
  18.3 0.0 copy-start.1
  18.3 27.1 %all_to_all.20 = bf16[8,16,4224]{2,1,0:T(8,128)(2,1)S(1)} all-to-all(bf16[8,16,4224]{2,1,0:T(8,128)(2,1)S(1)} %bitcast.19), channel_id=1, replica_groups={{0,6,12,2,8,14,4,10},{16,22,28,18,24,30,20,26},{32,38,44,34,40,46,36,42..., dimensions={0} | all-to-all | bytes 2162688 | tf_op jit(solution)/shard_map/all_to_all | solution.py:198
  45.4 1.1 dispatch.1
  46.6 0.0 copy-start
  46.6 23.1 %all_to_all.21 = bf16[16,16,4096]{2,1,0:T(8,128)(2,1)S(1)} all-to-all(bf16[16,16,4096]{2,1,0:T(8,128)(2,1)S(1)} %bitcast.23), channel_id=1, replica_groups={{0,112,224,80,192,48,160,16,128,240,96,208,64,176,32,144},{2,114,226,82..., dimensions={0} | all-to-all | bytes 4194304 | tf_op jit(solution)/shard_map/all_to_all | solution.py:198
  69.7 0.0 copy-done.1
  69.7 0.0 copy-done
  69.7 6.1 %expert.1 = bf16[256,4096]{1,0:T(8,128)(2,1)S(1)} custom-call(bf16[256,4096]{1,0:T(8,128)(2,1)S(1)} %bitcast.17, bf16[2048,768]{1,0:T(8,128)(2,1)S(1)} %bitcast.21, bf16[2048,768]{1,0:T(8,128)(2,1)S(1)} %bitcast.22, bf16[768,2048]{1,0:T(8,128)(2,1)} %bitcast.24), custom_call_target="tpu_custom_call" | custom-call | tf_op jit(solution)/shard_map/expert/pallas_call | solution.py:246
  75.9 20.5 %all_to_all.22 = bf16[16,16,4096]{2,1,0:T(8,128)(2,1)S(1)} all-to-all(bf16[16,16,4096]{2,1,0:T(8,128)(2,1)S(1)} %bitcast.18), channel_id=1, replica_groups={{0,112,224,80,192,48,160,16,128,240,96,208,64,176,32,144},{2,114,226,82..., dimensions={0} | all-to-all | bytes 4194304 | tf_op jit(solution)/shard_map/all_to_all | solution.py:198
  96.4 1.2 %combine.1 = bf16[128,4224]{1,0:T(8,128)(2,1)S(1)} custom-call(f32[128,256]{1,0:T(8,128)S(1)} %get-tuple-element.9.weight_ref, f32[128,256]{1,0:T(8,128)S(1)} %get-tuple-element.10.pick_ref, bf16[128,4224]{1,0:T(8,128)(2,1)S(1)} %bitcast.15, bf16[256,4096]{1,0:T(8,128)(2,1)S(1)} %bitcast.16), custom_call_target="tpu_custom_call" | custom-call | tf_op jit(solution)/shard_map/combine/pallas_call | solution.py:260
  97.6 20.7 %all_to_all.23.parts_ref = bf16[8,16,4224]{2,1,0:T(8,128)(2,1)S(1)} all-to-all(bf16[8,16,4224]{2,1,0:T(8,128)(2,1)S(1)} %bitcast.20), channel_id=1, replica_groups={{0,6,12,2,8,14,4,10},{16,22,28,18,24,30,20,26},{32,38,44,34,40,46,36,42..., dimensions={0} | all-to-all | bytes 2162688 | tf_op jit(solution)/shard_map/all_to_all | solution.py:198
  118.3 0.8 finish.1
Async XLA Ops:
  18.3 51.4 %copy-start.1 = (bf16[1,2048,768]{2,1,0:T(8,128)(2,1)S(1)}, bf16[1,2048,768]{2,1,0:T(8,128)(2,1)}, u32[]{:S(2)}) copy-start(bf16[1,2048,768]{2,1,0:T(8,128)(2,1)} %param.11) | copy-start | bytes 9437188
  46.6 23.2 %copy-start = (bf16[1,2048,768]{2,1,0:T(8,128)(2,1)S(1)}, bf16[1,2048,768]{2,1,0:T(8,128)(2,1)}, u32[]{:S(2)}) copy-start(bf16[1,2048,768]{2,1,0:T(8,128)(2,1)} %param.10) | copy-start | bytes 9437188

commit v7 on v6

--- a/solution.py
+++ b/solution.py
@@ -22,7 +22,7 @@
 BF = jnp.bfloat16
 F32 = jnp.float32
 COLUMNS = 512
-STAGGER = 17500
+STAGGER = 17000
 MIB = 1024 * 1024
 
 

time: 119 us -> 119 us (level)
  no operation moved by 1% of the time
where the time goes in v7:
time: 119 us
  blocking collectives  92 us (77%)
  Pallas kernels  26.5 us (22%)
    all_to_all x4, blocking collectives, exchange(): lax.all_to_all(blocks, ('dp', 'expert'), split_axis=0, concat_axis=0, til...  92 us
    pallas_call x1, Pallas kernels, local(): pl.pallas_call(pack_kernel, out_shape=pltpu.VMEM((LINE, total), BF), in_s...  17.2 us
    pallas_call x1, Pallas kernels, local(): pl.pallas_call(expert_kernel, out_shape=pltpu.VMEM((SLOTS, 2 * WIDTH), BF...  6.11 us

profile of v7, /device:TPU:1, one launch (start us, length us, event | category | flops | bytes accessed | tf_op | source)
XLA Modules:
  0.0 119.1 jit_solution(15312360074137256673)
XLA Ops:
  0.6 17.2 %pack.1 = bf16[128,4224]{1,0:T(8,128)(2,1)S(1)} custom-call(s32[1]{0:T(128)} %bitcast.depth_ref, bf16[16,2048]{1,0:T(8,128)(2,1)} %tokens_hbm.1, bf16[16,2048]{1,0:T(8,128)(2,1)} %cotangent_hbm.1, s32[8,16]{1,0:T(8,128)} %bitcast.25, f32[8,16]{1,0:T(8,128)} %bitcast.26), custom_call_target="tpu_custom_call" | custom-call | tf_op jit(solution)/shard_map/pack/pallas_call | solution.py:216
  17.8 0.0 copy-start.1
  17.8 27.1 %all_to_all.20 = bf16[8,16,4224]{2,1,0:T(8,128)(2,1)S(1)} all-to-all(bf16[8,16,4224]{2,1,0:T(8,128)(2,1)S(1)} %bitcast.19), channel_id=1, replica_groups={{0,6,12,2,8,14,4,10},{16,22,28,18,24,30,20,26},{32,38,44,34,40,46,36,42..., dimensions={0} | all-to-all | bytes 2162688 | tf_op jit(solution)/shard_map/all_to_all | solution.py:198
  44.9 1.1 dispatch.1
  46.1 0.0 copy-start
  46.1 23.2 %all_to_all.21 = bf16[16,16,4096]{2,1,0:T(8,128)(2,1)S(1)} all-to-all(bf16[16,16,4096]{2,1,0:T(8,128)(2,1)S(1)} %bitcast.23), channel_id=1, replica_groups={{0,112,224,80,192,48,160,16,128,240,96,208,64,176,32,144},{2,114,226,82..., dimensions={0} | all-to-all | bytes 4194304 | tf_op jit(solution)/shard_map/all_to_all | solution.py:198
  69.3 0.0 copy-done.1
  69.3 0.0 copy-done
  69.3 6.1 %expert.1 = bf16[256,4096]{1,0:T(8,128)(2,1)S(1)} custom-call(bf16[256,4096]{1,0:T(8,128)(2,1)S(1)} %bitcast.17, bf16[2048,768]{1,0:T(8,128)(2,1)S(1)} %bitcast.21, bf16[2048,768]{1,0:T(8,128)(2,1)S(1)} %bitcast.22, bf16[768,2048]{1,0:T(8,128)(2,1)} %bitcast.24), custom_call_target="tpu_custom_call" | custom-call | tf_op jit(solution)/shard_map/expert/pallas_call | solution.py:246
  75.4 20.5 %all_to_all.22 = bf16[16,16,4096]{2,1,0:T(8,128)(2,1)S(1)} all-to-all(bf16[16,16,4096]{2,1,0:T(8,128)(2,1)S(1)} %bitcast.18), channel_id=1, replica_groups={{0,112,224,80,192,48,160,16,128,240,96,208,64,176,32,144},{2,114,226,82..., dimensions={0} | all-to-all | bytes 4194304 | tf_op jit(solution)/shard_map/all_to_all | solution.py:198
  95.9 1.2 %combine.1 = bf16[128,4224]{1,0:T(8,128)(2,1)S(1)} custom-call(f32[128,256]{1,0:T(8,128)S(1)} %get-tuple-element.9.weight_ref, f32[128,256]{1,0:T(8,128)S(1)} %get-tuple-element.10.pick_ref, bf16[128,4224]{1,0:T(8,128)(2,1)S(1)} %bitcast.15, bf16[256,4096]{1,0:T(8,128)(2,1)S(1)} %bitcast.16), custom_call_target="tpu_custom_call" | custom-call | tf_op jit(solution)/shard_map/combine/pallas_call | solution.py:260
  97.2 21.2 %all_to_all.23.parts_ref = bf16[8,16,4224]{2,1,0:T(8,128)(2,1)S(1)} all-to-all(bf16[8,16,4224]{2,1,0:T(8,128)(2,1)S(1)} %bitcast.20), channel_id=1, replica_groups={{0,6,12,2,8,14,4,10},{16,22,28,18,24,30,20,26},{32,38,44,34,40,46,36,42..., dimensions={0} | all-to-all | bytes 2162688 | tf_op jit(solution)/shard_map/all_to_all | solution.py:198
  118.3 0.8 finish.1
Async XLA Ops:
  17.8 51.5 %copy-start.1 = (bf16[1,2048,768]{2,1,0:T(8,128)(2,1)S(1)}, bf16[1,2048,768]{2,1,0:T(8,128)(2,1)}, u32[]{:S(2)}) copy-start(bf16[1,2048,768]{2,1,0:T(8,128)(2,1)} %param.11) | copy-start | bytes 9437188
  46.1 23.2 %copy-start = (bf16[1,2048,768]{2,1,0:T(8,128)(2,1)S(1)}, bf16[1,2048,768]{2,1,0:T(8,128)(2,1)}, u32[]{:S(2)}) copy-start(bf16[1,2048,768]{2,1,0:T(8,128)(2,1)} %param.10) | copy-start | bytes 9437188
